TPU v7x, 32 devices: a whole 2x2x4 slice. The times are simulated.
32 devices in a mesh: row: 2 (over y), col: 16 (over z, x, core).
Axes of the slice: x: 2, y: 2, z: 4, core: 2. Of those that a mesh axis runs over, the one named last changes fastest.
Arguments:
- blocks: bfloat16 [128, 2048, 128], P('row', 'col'), may hold values from -0.1875 to 0.1875
- block_rows: int32 [2, 1024], P('row', 'col'), may hold values from 0 to 2047, as said below
- block_cols: int32 [2, 1024], P('row', 'col'), may hold values from 0 to 255
- counts: int32 [2, 16], P('row', 'col'), may hold values from 1 to 64, as said below
- start_vectors: float32 [32, 524288], P(None, ('row', 'col')), may hold values from -6 to 6
Outputs:
- vectors: float32 [32, 524288], P(None, ('row', 'col'))
Inputs may be any that keep to these rules, and one draw needn't show every extreme that they name: counts[r, c] is the number of live slots of grid position (r, c); in every draw some position has all 64 slots live. For every grid position (r, c) and every o < 16, exactly 4 of its 64 slots have block_rows[r, c * 64 + s] // 128 == o.
All inputs are finite; a program needn't handle non-finite values.
Results may differ from a plain program's by a relative error of at most 0.0036.
Values may be sent and summed in bfloat16 or wider, within the bound.
A program may use at most 256 MiB of HBM per device.

v0:
```python
import math

import jax
import jax.numpy as jnp
from jax import lax
from jax.sharding import PartitionSpec as P

N = 524288
ITERS = 2


def cholesky_lower(gram_matrix):
    matrix_order = gram_matrix.shape[0]
    positions = jnp.arange(matrix_order)

    def column_step(position, factor):
        before = (positions < position).astype(gram_matrix.dtype)
        target_row = lax.dynamic_index_in_dim(factor, position, 0, keepdims=False) * before
        column = lax.dynamic_index_in_dim(gram_matrix, position, 1, keepdims=False)
        residue = column - jnp.sum(factor * target_row[None, :], axis=1)
        on_diagonal = positions == position
        pivot_value = jnp.sqrt(jnp.sum(jnp.where(on_diagonal, residue, 0.0)))
        values = jnp.where(on_diagonal, pivot_value, residue / pivot_value)
        values = jnp.where(positions >= position, values, 0.0)
        return lax.dynamic_update_index_in_dim(factor, values, position, 1)

    return lax.fori_loop(0, matrix_order, column_step, jnp.zeros_like(gram_matrix))


def lower_inverse(lower_factor):
    matrix_order = lower_factor.shape[0]
    positions = jnp.arange(matrix_order)

    def row_step(position, inverse):
        lower_row = lax.dynamic_index_in_dim(lower_factor, position, 0, keepdims=False)
        before = (positions < position).astype(lower_factor.dtype)
        inner_sum = jnp.sum((lower_row * before)[:, None] * inverse, axis=0)
        unit_row = (positions == position).astype(lower_factor.dtype)
        pivot_value = jnp.sum(lower_row * unit_row)
        return lax.dynamic_update_index_in_dim(
            inverse, (unit_row - inner_sum) / pivot_value, position, 0
        )

    return lax.fori_loop(0, matrix_order, row_step, jnp.zeros_like(lower_factor))


def accumulate(blocks, rows_index, cols_index, live_count, row_panel, col_panel):
    slot_count, block_size = (blocks.shape[0], blocks.shape[1])
    vector_count = row_panel.shape[0]
    row_blocks = row_panel.reshape(vector_count, -1, block_size)
    col_blocks = col_panel.reshape(vector_count, -1, block_size)
    group_size = math.gcd(slot_count, 64)
    turn_count = (live_count + group_size - 1) // group_size
    slot_offsets = jnp.arange(group_size, dtype=jnp.int32)

    def one_group(turn_index, partial_sums):
        row_sums, col_sums = partial_sums
        first_slot = turn_index * group_size
        live_mask = (first_slot + slot_offsets < live_count).astype(jnp.float32)
        from_cols = jnp.take(col_blocks, cols_index, axis=1)
        from_rows = jnp.take(row_blocks, rows_index, axis=1)
        to_cols = jnp.einsum("kgi,gij->kgj", from_rows, blocks, preferred_element_type=jnp.float32)
        col_sums = col_sums.at[:, cols_index].add(to_cols * live_mask[None, :, None])
        to_rows = jnp.einsum("kgj,gij->kgi", from_cols, blocks, preferred_element_type=jnp.float32)
        row_sums = row_sums.at[:, rows_index].add(to_rows * live_mask[None, :, None])
        return (row_sums, col_sums)

    row_start = jnp.zeros(row_blocks.shape, jnp.float32)
    initial = (row_start, jnp.zeros(col_blocks.shape, jnp.float32))
    return lax.fori_loop(0, turn_count, one_group, initial)


def per_device(blocks, block_rows, block_cols, counts, start_vectors):
    live_count = counts[0, 0]
    rows_index = block_rows[0]
    cols_index = block_cols[0]
    vectors = start_vectors
    for iteration in range(ITERS):
        rounded = vectors.astype(jnp.bfloat16)
        vector_count = rounded.shape[0]
        col_panel = lax.all_gather(rounded, "row", axis=1, tiled=True)
        row_panel = lax.all_gather(rounded, "col", axis=1, tiled=True)
        row_sums, col_sums = accumulate(
            blocks, rows_index, cols_index, live_count, row_panel, col_panel
        )
        from_row_group = lax.psum_scatter(
            row_sums.reshape(vector_count, -1), "col", scatter_dimension=1, tiled=True
        )
        from_col_group = lax.psum_scatter(
            col_sums.reshape(vector_count, -1), "row", scatter_dimension=1, tiled=True
        )
        product = from_row_group + from_col_group
        local_gram = jnp.dot(
            product, product.T, precision=lax.Precision.HIGHEST, preferred_element_type=jnp.float32
        )
        gram_matrix = lax.psum(local_gram, ("row", "col")) / N
        inverse = lower_inverse(cholesky_lower(gram_matrix))
        vectors = jnp.dot(
            inverse, product, precision=lax.Precision.HIGHEST, preferred_element_type=jnp.float32
        )
    return vectors


def solution(mesh):
    placed = (
        P("row", "col", None),
        P("row", "col"),
        P("row", "col"),
        P("row", "col"),
        P(None, ("row", "col")),
    )
    return jax.shard_map(
        per_device, mesh=mesh, in_specs=placed, out_specs=P(None, ("row", "col")), check_vma=False
    )
```

profile of v0, /device:TPU:0, one launch (start us, length us, event | category | flops | bytes accessed | tf_op | source)
XLA Modules:
  0.0 1549.7 jit_solution(5209276909103308987)
XLA Ops:
  6.5 2.8 convert_element_type.66
  11.0 34.4 %all-gather.5.cloned.1.call-done = bf16[32,32768]{1,0:T(8,128)(2,1)} async-done(((bf16[32,16384]{1,0:T(8,128)(2,1)}), bf16[32,32768]{1,0:T(8,128)(2,1)}) %all-gather.5.cloned.1.call-update) | async-done | bytes 2097168 | tf_op jit(solution)/shard_map/all_gather | solution.py:81
  45.4 3.3 copy_bitcast_fusion.7
  48.6 2.2 gather_fusion
  50.9 2.2 fusion.34
  53.1 121.4 %all-gather.7.cloned.1.call-done = bf16[32,262144]{1,0:T(8,128)(2,1)} async-done(((bf16[32,16384]{1,0:T(8,128)(2,1)}), bf16[32,262144]{1,0:T(8,128)(2,1)}) %all-gather.7.cloned.1.call-update) | async-done | bytes 16777232 | tf_op jit(solution)/shard_map/all_gather | solution.py:82
  174.5 14.5 copy_bitcast_fusion.3
  189.0 6.4 gather_fusion.1
  195.4 1.7 fusion.32
  197.1 11.3 broadcast.314.clone
  208.4 2.6 broadcast.315.clone
  210.9 20.4 %while.90 = (s32[]{:T(128)}, f32[32,2048,128]{2,0,1:T(8,128)}, f32[32,256,128]{2,0,1:T(8,128)}, s32[]{:T(128)}, s32[64]{0:T(128)S(1)}, /*index=5*/s32[]{:T(128)}...) while((s32[]{:T(128)}, f32[32,2048,128]{2,0,1:T(8,128)}, ...), condition=%wide.region_3.6_spmd.clone, body=%wide.region_0.5_spmd.clone.sunk | while | flops 1049155 | bytes 10487937 | solution.py:70
  211.6 2.7 broadcast_multiply_fusion.8
  214.3 9.0 scatter_fusion
  223.3 8.0 scatter_fusion.1
  231.3 4.4 copy_bitcast_fusion.5
  235.8 22.6 %copy_bitcast_fusion.1 = f32[32,262144]{1,0:T(8,128)} fusion(f32[32,2048,128]{2,0,1:T(8,128)} %get-tuple-element.609), kind=kLoop, calls=%fused_computation.69 | loop fusion | bytes 67108864 | tf_op jit(solution)/shard_map/reshape | solution.py:87
  258.5 29.9 %reduce-scatter.7.cloned.1.call-done = f32[32,16384]{1,0:T(8,128)} async-done(((f32[32,32768]{1,0:T(8,128)}), f32[32,16384]{1,0:T(8,128)}) %reduce-scatter.7.cloned.1.call-update) | async-done | bytes 2097168 | tf_op jit(solution)/shard_map/reduce_scatter | solution.py:89
  288.4 337.4 %reduce-scatter.5.cloned.1.call-done = f32[32,16384]{1,0:T(8,128)} async-done(((f32[32,262144]{1,0:T(8,128)}), f32[32,16384]{1,0:T(8,128)}) %reduce-scatter.5.cloned.1.call-update) | async-done | bytes 2097168 | tf_op jit(solution)/shard_map/reduce_scatter | solution.py:86
  625.8 2.4 add.220
  629.6 1.8 fusion.52
  631.4 39.0 %psum.14 = f32[32,32]{1,0:T(8,128)S(1)} all-reduce(f32[32,32]{1,0:T(8,128)S(1)} %fusion.52), channel_id=1, replica_groups=mesh['row'=2,'col'=16] {'row','col'}, use_global_device_ids=true, to_apply=%region_6.9 | all-reduce | flops 1024 | bytes 8192 | tf_op jit(solution)/shard_map/psum | solution.py:96
  670.5 58.1 %while.92 = (s32[]{:T(128)}, f32[32,32]{1,0:T(8,128)S(1)}, f32[32,32]{0,1:T(8,128)S(1)}, s32[]{:T(128)}, s32[]{:T(128)}) while((s32[]{:T(128)}, f32[32,32]{1,0:T(8,128)S(1)}, f32[32,32]{0,1:T(8,128)S(1)}, s32[]{:T(128)}, s32[]{:T(128)}) %tuple.192), condition=%wide.region_10.13_spmd.clone.clone, body=%wide.region_7.12_spmd.clone.clone.sunk | while | flops 2401 | bytes 8913 | solution.py:27
  728.6 49.0 %while.93 = (s32[]{:T(128)}, f32[32,32]{1,0:T(8,128)S(1)}, f32[32,32]{1,0:T(8,128)S(1)}, s32[]{:T(128)}, s32[]{:T(128)}) while((s32[]{:T(128)}, f32[32,32]{1,0:T(8,128)S(1)}, f32[32,32]{1,0:T(8,128)S(1)}, s32[]{:T(128)}, s32[]{:T(128)}) %tuple.195), condition=%wide.region_14.17_spmd.clone.clone, body=%wide.region_11.16_spmd.clone.clone.sunk | while | flops 2305 | bytes 6221 | solution.py:44
  777.6 4.4 convolution_convert_fusion
  782.8 32.2 %all-gather.9.cloned.1.call-done = bf16[32,32768]{1,0:T(8,128)(2,1)} async-done(((bf16[32,16384]{1,0:T(8,128)(2,1)}), bf16[32,32768]{1,0:T(8,128)(2,1)}) %all-gather.9.cloned.1.call-update) | async-done | bytes 2097168 | tf_op jit(solution)/shard_map/all_gather | solution.py:81
  815.1 3.3 copy_bitcast_fusion.6
  818.4 2.2 gather_fusion.2
  820.6 2.2 fusion.30
  822.8 121.5 %all-gather.11.cloned.1.call-done = bf16[32,262144]{1,0:T(8,128)(2,1)} async-done(((bf16[32,16384]{1,0:T(8,128)(2,1)}), bf16[32,262144]{1,0:T(8,128)(2,1)}) %all-gather.11.cloned.1.call-update) | async-done | bytes 16777232 | tf_op jit(solution)/shard_map/all_gather | solution.py:82
  944.3 14.5 copy_bitcast_fusion.2
  958.8 6.4 gather_fusion.3
  966.9 11.3 broadcast.314
  978.2 2.6 broadcast.315
  980.8 20.4 %while.91 = (s32[]{:T(128)}, f32[32,2048,128]{2,0,1:T(8,128)}, f32[32,256,128]{2,0,1:T(8,128)}, s32[]{:T(128)}, s32[64]{0:T(128)S(1)}, /*index=5*/s32[]{:T(128)}...) while((s32[]{:T(128)}, f32[32,2048,128]{2,0,1:T(8,128)}, ...), condition=%wide.region_18.21_spmd.clone, body=%wide.region_15.20_spmd.clone.sunk | while | flops 1049155 | bytes 10487937 | solution.py:70
  981.4 2.7 broadcast_multiply_fusion.9
  984.1 9.0 scatter_fusion.2
  993.1 8.0 scatter_fusion.3
  1001.1 4.4 copy_bitcast_fusion.4
  1005.6 22.6 %copy_bitcast_fusion = f32[32,262144]{1,0:T(8,128)} fusion(f32[32,2048,128]{2,0,1:T(8,128)} %get-tuple-element.613), kind=kLoop, calls=%fused_computation.68 | loop fusion | bytes 67108864 | tf_op jit(solution)/shard_map/reshape | solution.py:87
  1028.2 30.0 %reduce-scatter.11.cloned.1.call-done = f32[32,16384]{1,0:T(8,128)} async-done(((f32[32,32768]{1,0:T(8,128)}), f32[32,16384]{1,0:T(8,128)}) %reduce-scatter.11.cloned.1.call-update) | async-done | bytes 2097168 | tf_op jit(solution)/shard_map/reduce_scatter | solution.py:89
  1058.2 337.0 %reduce-scatter.9.cloned.1.call-done = f32[32,16384]{1,0:T(8,128)} async-done(((f32[32,262144]{1,0:T(8,128)}), f32[32,16384]{1,0:T(8,128)}) %reduce-scatter.9.cloned.1.call-update) | async-done | bytes 2097168 | tf_op jit(solution)/shard_map/reduce_scatter | solution.py:86
  1395.2 2.4 add.221
  1399.0 1.8 fusion.53
  1400.7 39.0 %psum.15 = f32[32,32]{1,0:T(8,128)S(1)} all-reduce(f32[32,32]{1,0:T(8,128)S(1)} %fusion.53), channel_id=1, replica_groups=mesh['row'=2,'col'=16] {'row','col'}, use_global_device_ids=true, to_apply=%region_21.24 | all-reduce | flops 1024 | bytes 8192 | tf_op jit(solution)/shard_map/psum | solution.py:96
  1439.8 53.9 %while.94 = (s32[]{:T(128)}, f32[32,32]{1,0:T(8,128)S(1)}, f32[32,32]{0,1:T(8,128)S(1)}, s32[]{:T(128)}, s32[]{:T(128)}) while((s32[]{:T(128)}, f32[32,32]{1,0:T(8,128)S(1)}, f32[32,32]{0,1:T(8,128)S(1)}, s32[]{:T(128)}, s32[]{:T(128)}) %tuple.201), condition=%wide.region_25.28_spmd.clone.clone, body=%wide.region_22.27_spmd.clone.clone.sunk | while | flops 2401 | bytes 8913 | solution.py:27
  1493.8 44.3 %while.95 = (s32[]{:T(128)}, f32[32,32]{1,0:T(8,128)S(1)}, f32[32,32]{1,0:T(8,128)S(1)}, s32[]{:T(128)}, s32[]{:T(128)}) while((s32[]{:T(128)}, f32[32,32]{1,0:T(8,128)S(1)}, f32[32,32]{1,0:T(8,128)S(1)}, s32[]{:T(128)}, s32[]{:T(128)}) %tuple.204), condition=%wide.region_29.32_spmd.clone.clone, body=%wide.region_26.31_spmd.clone.clone.sunk | while | flops 2305 | bytes 6221 | solution.py:44
  1538.1 4.8 fusion.54
  (685 shorter events, 164.6 us)
Async XLA Ops:
  6.5 44.4 %copy-start = (bf16[64,128,128]{2,1,0:T(8,128)(2,1)S(1)}, bf16[64,128,128]{2,1,0:T(8,128)(2,1)}, u32[]{:S(2)}) copy-start(bf16[64,128,128]{2,1,0:T(8,128)(2,1)} %param.21) | copy-start | bytes 6291460
  6.5 4.3 copy-start.3
  6.5 4.4 copy-start.4
  6.5 38.8 %all-gather.5.cloned.1.call-start = ((), (), s32[]{:S(2)}) async-start(), calls=%async_computation.4 | async-start | bytes 3145728 | tf_op jit(solution)/shard_map/all_gather | solution.py:81
  9.4 165.1 %all-gather.7.cloned.1.call-start = ((), (), s32[]{:S(2)}) async-start(), calls=%async_computation.5 | async-start | bytes 17825792 | tf_op jit(solution)/shard_map/all_gather | solution.py:82
  10.2 278.3 %reduce-scatter.7.cloned.1.call-start = ((), (), s32[]{:S(2)}) async-start(), calls=%async_computation.7 | async-start | bytes 6291456 | tf_op jit(solution)/shard_map/reduce_scatter | solution.py:89
  235.8 390.1 %reduce-scatter.5.cloned.1.call-start = ((), (), s32[]{:S(2)}) async-start(), calls=%async_computation.6 | async-start | bytes 35651584 | tf_op jit(solution)/shard_map/reduce_scatter | solution.py:86
  258.4 556.6 %all-gather.9.cloned.1.call-start = ((), (), s32[]{:S(2)}) async-start(), calls=%async_computation.8 | async-start | bytes 3145728 | tf_op jit(solution)/shard_map/all_gather | solution.py:81
  628.3 1.3 copy-start.2
  782.0 162.3 %all-gather.11.cloned.1.call-start = ((), (), s32[]{:S(2)}) async-start(), calls=%async_computation.9 | async-start | bytes 17825792 | tf_op jit(solution)/shard_map/all_gather | solution.py:82
  782.6 275.6 %reduce-scatter.11.cloned.1.call-start = ((), (), s32[]{:S(2)}) async-start(), calls=%async_computation.11 | async-start | bytes 6291456 | tf_op jit(solution)/shard_map/reduce_scatter | solution.py:89
  1005.6 389.6 %reduce-scatter.9.cloned.1.call-start = ((), (), s32[]{:S(2)}) async-start(), calls=%async_computation.10 | async-start | bytes 35651584 | tf_op jit(solution)/shard_map/reduce_scatter | solution.py:86
  1397.6 1.4 copy-start.1
Sparse Core Ops, SparseCore 0:
  9.5 35.8 all-gather.4
  47.6 126.9 all-gather.6
  235.9 52.4 reduce-scatter.6
  293.1 332.6 reduce-scatter.4
  782.1 32.8 all-gather.8
  817.4 126.9 all-gather.10
  1005.7 52.4 reduce-scatter.10
  1062.5 332.6 reduce-scatter.8
where the time goes:
time: 1550 us
  waiting for transfers between devices  1050 us (68%)
  other arithmetic  189 us (12%)
  local copies, waits for them, and re-layouts  153 us (10%)
  blocking collectives  78 us (5%)
  loops' own time  48.3 us (3%)
  matrix products  20.5 us (1%)
    reduce_scatter x2, waiting for transfers between devices, per_device(): lax.psum_scatter(row_sums.reshape(vector_count, -1), 'col', scatter_dimen...  674 us
    all_gather x2, waiting for transfers between devices, per_device(): row_panel = lax.all_gather(rounded, 'col', axis=1, tiled=True)  243 us
    psum x2, blocking collectives, per_device(): gram_matrix = lax.psum(local_gram, ('row', 'col')) / N  78 us
    all_gather x2, waiting for transfers between devices, per_device(): col_panel = lax.all_gather(rounded, 'row', axis=1, tiled=True)  66.7 us
    reduce_scatter x2, waiting for transfers between devices, per_device(): lax.psum_scatter(col_sums.reshape(vector_count, -1), 'row', scatter_dimen...  59.9 us
    another operation x2, loops' own time, cholesky_lower(): lax.fori_loop(0, matrix_order, column_step, jnp.zeros_like(gram_matrix))  46.9 us
    reshape x2, local copies, waits for them, and re-layouts, per_device(): row_sums.reshape(vector_count, -1)  45.2 us
    reduce_sum x64, other arithmetic, column_step(): pivot_value = jnp.sqrt(jnp.sum(jnp.where(on_diagonal, residue, 0.0)))  42.8 us
  transfers between devices with their start and end apart: 8, of which 8 were waited for; matrix products, arithmetic and copies ran while one was open for 4% of the time, Pallas kernels for 0%

commit v1 on v0

v1 whole, which is shorter than its diff:
```python
import functools

import jax
import jax.numpy as jnp
from jax import lax
from jax.experimental import pallas as pl
from jax.experimental.pallas import tpu as pltpu
from jax.sharding import PartitionSpec as P

ITERS = 2
MESH = pl.DeviceIdType.MESH
ANY = pl.BlockSpec(memory_space=pl.ANY)
VMEM = pl.BlockSpec(memory_space=pltpu.VMEM)
SMEM = pl.BlockSpec(memory_space=pltpu.SMEM)
VMEM_BYTES = 48 << 20


def greet(n_row, n_col):
    my_row, my_col = lax.axis_index("row"), lax.axis_index("col")
    barrier = pltpu.get_barrier_semaphore()
    for d in range(1, n_col):
        peer = lax.rem(my_col + d, n_col)
        pl.semaphore_signal(barrier, inc=1, device_id=(my_row, peer), device_id_type=MESH)
    for d in range(1, n_row):
        peer = lax.rem(my_row + d, n_row)
        pl.semaphore_signal(barrier, inc=1, device_id=(peer, my_col), device_id_type=MESH)
    pl.semaphore_wait(barrier, n_col + n_row - 2)
    return my_row, my_col


def exchange_kernel(n_row, n_col, c_src, r_src, c_dst, r_dst, own, c_send, c_recv, r_send, r_recv):
    my_row, my_col = greet(n_row, n_col)
    shared = r_src.shape[0] == 1
    copies = []
    for d in range(1, n_row):
        peer = lax.rem(my_row + d, n_row)
        copies.append(
            pltpu.make_async_remote_copy(
                src_ref=r_src.at[0 if shared else peer],
                dst_ref=r_dst.at[my_row],
                send_sem=r_send.at[d],
                recv_sem=r_recv.at[d],
                device_id=(peer, my_col),
                device_id_type=MESH,
            )
        )
    for d in range(1, n_col):
        peer = lax.rem(my_col + d, n_col)
        copies.append(
            pltpu.make_async_remote_copy(
                src_ref=c_src.at[peer],
                dst_ref=c_dst.at[my_col],
                send_sem=c_send.at[d],
                recv_sem=c_recv.at[d],
                device_id=(my_row, peer),
                device_id_type=MESH,
            )
        )
    copies.append(pltpu.make_async_copy(c_src.at[my_col], c_dst.at[my_col], own.at[0]))
    copies.append(
        pltpu.make_async_copy(r_src.at[0 if shared else my_row], r_dst.at[my_row], own.at[1])
    )
    for copy in copies:
        copy.start()
    for copy in copies:
        copy.wait()


def exchange(n_row, n_col, collective_id, c_src, r_src):
    return pl.pallas_call(
        functools.partial(exchange_kernel, n_row, n_col),
        out_shape=(
            jax.ShapeDtypeStruct(c_src.shape, c_src.dtype),
            jax.ShapeDtypeStruct((n_row,) + r_src.shape[1:], r_src.dtype),
        ),
        in_specs=[ANY, ANY],
        out_specs=(ANY, ANY),
        scratch_shapes=[
            pltpu.SemaphoreType.DMA((2,)),
            pltpu.SemaphoreType.DMA((n_col,)),
            pltpu.SemaphoreType.DMA((n_col,)),
            pltpu.SemaphoreType.DMA((n_row,)),
            pltpu.SemaphoreType.DMA((n_row,)),
        ],
        compiler_params=pltpu.CompilerParams(collective_id=collective_id, has_side_effects=True),
    )(c_src, r_src)


def split(value):
    high = value.astype(jnp.bfloat16)
    return high, (value - high.astype(jnp.float32)).astype(jnp.bfloat16)


def inverse_stack(inverse):
    high, low = split(inverse)
    return jnp.concatenate([high, low, high, low], axis=1)


def apply_inverse(stacked, product):
    high, low = split(product)
    parts = jnp.concatenate([high, high, low, low], axis=0)
    return jnp.dot(stacked, parts, preferred_element_type=jnp.float32)


def pack_kernel(first, wanted, all_cols, source, *rest):
    if first:
        c_out, r_out, held = rest
        for b in range(held.shape[0]):
            held[b] = source[:, b * 128 : (b + 1) * 128].astype(jnp.bfloat16)
    else:
        inverse, c_out, r_out, held = rest
        stacked = inverse_stack(inverse[...])

        def round_block(b, carry):
            held[b] = apply_inverse(stacked, source[b]).astype(jnp.bfloat16)
            return carry

        lax.fori_loop(0, held.shape[0], round_block, 0, unroll=8)
    panel = held.shape[0]
    base = lax.axis_index("row") * panel

    def one_c(t, carry):
        c_out[t] = held[wanted[t]]
        return carry

    lax.fori_loop(0, c_out.shape[0], one_c, 0, unroll=8)
    for p in range(all_cols.shape[0]):

        def one_r(t, carry):
            r_out[p, t] = held[jnp.clip(all_cols[p, t] - base, 0, panel - 1)]
            return carry

        lax.fori_loop(0, r_out.shape[1], one_r, 0, unroll=8)


def multiply_kernel(panel, perm, cols, live, blocks, from_rows, from_cols, to_rows, to_cols):
    def one_slot(t, carry):
        block = blocks[perm[t]]
        alive = live[t] > 0
        x_row = from_rows[t]
        x_col = from_cols[cols[t] // panel, t]
        row_product = lax.dot_general(
            x_col, block, (((1,), (1,)), ((), ())), preferred_element_type=jnp.float32
        )
        col_product = jnp.dot(x_row, block, preferred_element_type=jnp.float32)
        to_rows[t] = jnp.where(alive, row_product, 0.0).astype(jnp.bfloat16)
        to_cols[t] = jnp.where(alive, col_product, 0.0).astype(jnp.bfloat16)
        return carry

    lax.fori_loop(0, blocks.shape[0], one_slot, 0, unroll=8)


def sum_kernel(wanted, all_cols, row_terms, col_terms, product, gram):
    panel, vectors = product.shape[0], product.shape[1]
    base = lax.axis_index("row") * panel
    product[...] = jnp.zeros_like(product)

    def one_row(t, carry):
        at = wanted[t]
        product[at] = product[at] + row_terms[t].astype(jnp.float32)
        return carry

    lax.fori_loop(0, row_terms.shape[0], one_row, 0, unroll=4)
    for p in range(all_cols.shape[0]):

        def one_col(t, carry):
            at = all_cols[p, t] - base

            @pl.when((at >= 0) & (at < panel))
            def _():
                product[at] = product[at] + col_terms[p, t].astype(jnp.float32)

            return carry

        lax.fori_loop(0, col_terms.shape[1], one_col, 0, unroll=4)

    def one_gram(b, total):
        high, low = split(product[b])
        parts = jnp.concatenate([high, low], axis=0)
        return total + lax.dot_general(
            parts, parts, (((1,), (1,)), ((), ())), preferred_element_type=jnp.float32
        )

    total = lax.fori_loop(
        0, panel, one_gram, jnp.zeros((2 * vectors, 2 * vectors), jnp.float32), unroll=8
    )
    upper = total[:vectors] + total[vectors:]
    full = upper[:, :vectors] + upper[:, vectors:]
    gram[...] = jnp.concatenate([full[8 * i : 8 * i + 8] for i in range(vectors // 8)], axis=1)


def factor_kernel(
    n_row, n_col, order, gram, inverse, row_in, row_sum, col_in, r_send, r_recv, c_send, c_recv
):
    my_row, my_col = greet(n_row, n_col)
    copies = []
    for d in range(1, n_row):
        peer = lax.rem(my_row + d, n_row)
        copies.append(
            pltpu.make_async_remote_copy(
                src_ref=gram,
                dst_ref=row_in.at[my_row],
                send_sem=r_send.at[d],
                recv_sem=r_recv.at[d],
                device_id=(peer, my_col),
                device_id_type=MESH,
            )
        )
    for copy in copies:
        copy.start()
    row_in[my_row] = gram[...]
    for copy in copies:
        copy.wait()
    row_sum[...] = jnp.sum(row_in[...], axis=0)
    copies = []
    for d in range(1, n_col):
        peer = lax.rem(my_col + d, n_col)
        copies.append(
            pltpu.make_async_remote_copy(
                src_ref=row_sum,
                dst_ref=col_in.at[my_col],
                send_sem=c_send.at[d],
                recv_sem=c_recv.at[d],
                device_id=(my_row, peer),
                device_id_type=MESH,
            )
        )
    for copy in copies:
        copy.start()
    col_in[my_col] = row_sum[...]
    for copy in copies:
        copy.wait()
    packed = jnp.sum(col_in[...], axis=0) / order
    size = inverse.shape[0]
    full = jnp.concatenate([packed[:, size * i : size * (i + 1)] for i in range(size // 8)], axis=0)
    rows = lax.broadcasted_iota(jnp.int32, (size, size), 0)
    lanes = lax.broadcasted_iota(jnp.int32, (size, size), 1)
    work = jnp.concatenate([full, (rows == lanes).astype(jnp.float32)], axis=1)
    row_ids = lax.broadcasted_iota(jnp.int32, (size, 2 * size), 0)
    for j in range(size):
        scale = 1.0 / jnp.sqrt(work[j : j + 1, j : j + 1])
        pivot_row = work[j : j + 1, :] * scale
        factors = work[:, j : j + 1] * scale
        work = jnp.where(
            row_ids > j, work - factors * pivot_row, jnp.where(row_ids == j, pivot_row, work)
        )
    inverse[...] = work[:, size:]


def finish_kernel(source, inverse, out):
    stacked = inverse_stack(inverse[...])
    for b in range(source.shape[0]):
        out[:, b * 128 : (b + 1) * 128] = apply_inverse(stacked, source[b])


def local_params():
    return pltpu.CompilerParams(vmem_limit_bytes=VMEM_BYTES)


def per_device(n_row, n_col, blocks, block_rows, block_cols, counts, start_vectors):
    slots, size = blocks.shape[0], blocks.shape[1]
    vectors, width = start_vectors.shape
    panel = width // size
    share = slots // n_col
    bf16, f32 = jnp.bfloat16, jnp.float32
    shape = jax.ShapeDtypeStruct

    rows, cols, ids = block_rows[0], block_cols[0], jnp.arange(slots, dtype=jnp.int32)
    owner = rows // panel
    earlier = (owner[None, :] == owner[:, None]) & (ids[None, :] < ids[:, None])
    place = owner * share + jnp.sum(earlier.astype(jnp.int32), axis=1)
    here = (place[None, :] == ids[:, None]).astype(jnp.int32)
    perm = jnp.sum(here * ids[None, :], axis=1)
    rows = jnp.sum(here * rows[None, :], axis=1)
    cols = jnp.sum(here * cols[None, :], axis=1)
    live = (perm < counts[0, 0]).astype(jnp.int32)

    row_ask = jnp.pad((rows % panel).reshape(n_col, 1, share), ((0, 0), (0, 7), (0, 128 - share)))
    col_ask = jnp.pad(cols.reshape(1, 1, slots), ((0, 0), (0, 7), (0, 128 - slots)))
    row_got, col_got = exchange(n_row, n_col, 0, row_ask, col_ask)
    wanted = row_got[:, 0, :share].reshape(slots)
    all_cols = col_got[:, 0, :slots]

    product = inverse = None
    for iteration in range(ITERS):
        first = iteration == 0
        sources = (start_vectors,) if first else (product, inverse)
        c_src, r_src = pl.pallas_call(
            functools.partial(pack_kernel, first),
            out_shape=(
                shape((slots, vectors, size), bf16),
                shape((n_row, slots, vectors, size), bf16),
            ),
            in_specs=[SMEM, SMEM] + [VMEM] * len(sources),
            out_specs=(VMEM, VMEM),
            scratch_shapes=[pltpu.VMEM((panel, vectors, size), bf16)],
            compiler_params=local_params(),
        )(wanted, all_cols, *sources)
        from_rows, from_cols = exchange(
            n_row, n_col, 1, c_src.reshape(n_col, share, vectors, size), r_src
        )
        to_rows, to_cols = pl.pallas_call(
            functools.partial(multiply_kernel, panel),
            out_shape=(shape((slots, vectors, size), bf16),) * 2,
            in_specs=[SMEM] * 3 + [VMEM] * 3,
            out_specs=(VMEM, VMEM),
            compiler_params=local_params(),
        )(perm, cols, live, blocks, from_rows.reshape(slots, vectors, size), from_cols)
        row_terms, col_terms = exchange(
            n_row, n_col, 2, to_rows.reshape(n_col, share, vectors, size), to_cols[None]
        )
        product, gram = pl.pallas_call(
            sum_kernel,
            out_shape=(shape((panel, vectors, size), f32), shape((8, vectors * vectors // 8), f32)),
            in_specs=[SMEM, SMEM, VMEM, VMEM],
            out_specs=(VMEM, VMEM),
            compiler_params=local_params(),
        )(wanted, all_cols, row_terms.reshape(slots, vectors, size), col_terms)
        packed = pltpu.VMEM(gram.shape, f32)
        inverse = pl.pallas_call(
            functools.partial(factor_kernel, n_row, n_col, float(n_row * n_col * width)),
            out_shape=shape((vectors, vectors), f32),
            in_specs=[VMEM],
            out_specs=VMEM,
            scratch_shapes=[
                pltpu.VMEM((n_row,) + gram.shape, f32),
                packed,
                pltpu.VMEM((n_col,) + gram.shape, f32),
                pltpu.SemaphoreType.DMA((n_row,)),
                pltpu.SemaphoreType.DMA((n_row,)),
                pltpu.SemaphoreType.DMA((n_col,)),
                pltpu.SemaphoreType.DMA((n_col,)),
            ],
            compiler_params=pltpu.CompilerParams(collective_id=3, has_side_effects=True),
        )(gram)
    return pl.pallas_call(
        finish_kernel,
        out_shape=shape((vectors, width), f32),
        in_specs=[VMEM, VMEM],
        out_specs=VMEM,
        compiler_params=local_params(),
    )(product, inverse)


def solution(mesh):
    placed = (
        P("row", "col", None),
        P("row", "col"),
        P("row", "col"),
        P("row", "col"),
        P(None, ("row", "col")),
    )
    return jax.shard_map(
        functools.partial(per_device, mesh.shape["row"], mesh.shape["col"]),
        mesh=mesh,
        in_specs=placed,
        out_specs=P(None, ("row", "col")),
        check_vma=False,
    )
```

time: 1550 us -> 178 us (0.11)
  waiting for transfers between devices: 1050 us -> 0 us
  other arithmetic: 189 us -> 3.04 us
  Pallas kernels: 0 us -> 147 us
  local copies, waits for them, and re-layouts: 153 us -> 25.8 us
  blocking collectives: 78 us -> 0 us
  loops' own time: 48.3 us -> 0 us
  matrix products: 20.5 us -> 0 us
    reduce_scatter x4 -> x0, waiting for transfers between devices: 734 us -> none  [the longest x2 674 us: per_device(): lax.psum_scatter(row_sums.reshape(vector_count, -1), 'col', scatter_dimen...]
    all_gather x4 -> x0, waiting for transfers between devices: 310 us -> none  [the longest x2 243 us: per_device(): row_panel = lax.all_gather(rounded, 'col', axis=1, tiled=True)]
    pallas_call x0 -> x14, Pallas kernels: none -> 147 us  [the longest x5 93.1 us: exchange(): pl.pallas_call(functools.partial(exchange_kernel, n_row, n_col), out_shap...]
    reduce_sum x256 -> x2, other arithmetic: 97.3 us -> 1 us  [the longest x1 0.82 us: per_device(): perm = jnp.sum(here * ids[None, :], axis=1)]
    reshape x8 -> x0, local copies, waits for them, and re-layouts: 89.5 us -> none  [the longest x2 45.2 us: per_device(): row_sums.reshape(vector_count, -1)]
    psum x2 -> x0, blocking collectives: 78 us -> none  [per_device(): gram_matrix = lax.psum(local_gram, ('row', 'col')) / N]
    another operation x6 -> x0, loops' own time: 48.3 us -> none  [the longest x2 46.9 us: cholesky_lower(): lax.fori_loop(0, matrix_order, column_step, jnp.zeros_like(gram_matrix))]
    div x66 -> x0, other arithmetic: 42 us -> none  [the longest x64 42 us: row_step(): (unit_row - inner_sum) / pivot_value]
  transfers between devices with their start and end apart: 8 -> 0, of which waited for: 8 -> 0; matrix products, arithmetic and copies ran while one was open for 4% -> 0% of each run, Pallas kernels for 0% -> 0%
where the time goes in v1:
time: 178 us; the launch traced here: 177 us
  Pallas kernels  147 us (83%)
  local copies, waits for them, and re-layouts  25.8 us (14%)
  other arithmetic  3.04 us (2%)
    pallas_call x5, Pallas kernels, exchange(): pl.pallas_call(functools.partial(exchange_kernel, n_row, n_col), out_shap...  93.1 us
    pallas_call x2, Pallas kernels, per_device(): pl.pallas_call(functools.partial(factor_kernel, n_row, n_col, float(n_row...  27.7 us
    unnamed x48, local copies, waits for them, and re-layouts  22.9 us
    pallas_call x2, Pallas kernels, per_device(): pl.pallas_call(sum_kernel, out_shape=(shape((panel, vectors, size), f32),...  11.9 us
    pallas_call x2, Pallas kernels, per_device(): pl.pallas_call(functools.partial(multiply_kernel, panel), out_shape=(shap...  6.42 us
    pallas_call x2, Pallas kernels, per_device(): pl.pallas_call(functools.partial(pack_kernel, first), out_shape=(shape((s...  5.42 us

profile of v1, /device:TPU:0, one launch (start us, length us, event | category | flops | bytes accessed | tf_op | source)
XLA Modules:
  0.0 177.0 jit_solution(7194150584359158995)
XLA Ops:
  0.8 0.7 and_select_fusion.1
  1.5 0.7 fusion.3
  2.1 0.2 convert_reduce_fusion
  2.3 0.7 fusion.2
  3.0 0.8 select_reduce_fusion
  3.8 0.6 pad.9.r_src
  4.4 0.1 reduce_sum.43
  4.5 0.6 pad.8.c_src
  5.2 9.8 %shard_map.55 = (s32[16,8,128]{2,1,0:T(8,128)}, s32[2,8,128]{2,1,0:T(8,128)}) custom-call(s32[16,8,128]{2,1,0:T(8,128)} %pad.8.c_src, s32[1,8,128]{2,1,0:T(8,128)} %pad.9.r_src), custom_call_target="tpu_custom_call" | custom-call | tf_op jit(solution)/shard_map/pallas_call | solution.py:70
  15.0 0.9 slice_reduce_fusion
  15.8 0.1 reshape_squeeze.3.wanted
  15.9 0.7 slice.7
  16.6 1.6 copy-done.1
  18.2 1.2 shard_map.56
  19.5 1.0 copy-done.9
  20.4 0.8 copy-done.13
  21.2 21.9 %shard_map.57 = (bf16[16,4,32,128]{3,2,1,0:T(8,128)(2,1)}, bf16[2,64,32,128]{3,2,1,0:T(8,128)(2,1)}) custom-call(bf16[16,4,32,128]{3,2,1,0:T(8,128)(2,1)} %bitcast.29, bf16[2,64,32,128]{3,2,1,0:T(8,128)(2,1)} %copy-done.9), custom_call_target="tpu_custom_call" | custom-call | tf_op jit(solution)/shard_map/pallas_call | solution.py:70
  43.2 1.2 copy-done.5
  44.4 1.0 copy-done.19
  45.4 3.2 %shard_map.58 = (bf16[64,32,128]{2,1,0:T(8,128)(2,1)S(1)}, bf16[64,32,128]{2,1,0:T(8,128)(2,1)S(1)}) custom-call(s32[64]{0:T(128)S(1)} %get-tuple-element.49.perm, s32[64]{0:T(128)S(1)} %get-tuple-element.50.cols, s32[64]{0:T(128)S(1)} %compare_convert_fusion.live, bf16[64,128,128]{2,1,0:T(8,128)(2,1)S(1)} %copy-done, bf16[64,32,128]{2,1,0:T(8,128)(2,1)S(1)} %bitcast.35, ...), custom_call_target="tpu_custom_call" | custom-call | tf_op jit(solution)/shard_map/pallas_call | solution.py:302
  48.7 0.8 copy-done.16
  49.5 0.8 copy-done.17
  50.3 19.9 %shard_map.59 = (bf16[16,4,32,128]{3,2,1,0:T(8,128)(2,1)}, bf16[2,64,32,128]{3,2,1,0:T(8,128)(2,1)}) custom-call(bf16[16,4,32,128]{3,2,1,0:T(8,128)(2,1)} %bitcast.32, bf16[1,64,32,128]{3,2,1,0:T(8,128)(2,1)} %bitcast.33), custom_call_target="tpu_custom_call" | custom-call | tf_op jit(solution)/shard_map/pallas_call | solution.py:70
  70.1 1.2 copy-done.7
  71.3 1.0 copy-done.11
  72.4 6.0 %shard_map.60 = (f32[128,32,128]{2,1,0:T(8,128)S(1)}, f32[8,128]{1,0:T(8,128)S(1)}) custom-call(s32[64]{0:T(128)S(1)} %reshape_squeeze.3.wanted, s32[2,64]{1,0:T(2,128)S(1)} %bitcast.37, bf16[64,32,128]{2,1,0:T(8,128)(2,1)S(1)} %bitcast.27, bf16[2,64,32,128]{3,2,1,0:T(8,128)(2,1)S(1)} %copy-done.7), custom_call_target="tpu_custom_call" | custom-call | tf_op jit(solution)/shard_map/pallas_call | solution.py:312
  78.3 1.3 copy-done.2
  79.7 0.6 copy-done.23
  80.3 13.5 %shard_map.61.rest_0_ = f32[32,32]{1,0:T(8,128)} custom-call(f32[8,128]{1,0:T(8,128)} %copy-done.23), custom_call_target="tpu_custom_call" | custom-call | tf_op jit(solution)/shard_map/pallas_call | solution.py:320
  93.8 1.6 copy-done.3
  95.4 0.7 copy-done.20
  96.1 4.2 %shard_map.62 = (bf16[64,32,128]{2,1,0:T(8,128)(2,1)S(1)}, bf16[2,64,32,128]{3,2,1,0:T(8,128)(2,1)S(1)}) custom-call(s32[64]{0:T(128)S(1)} %reshape_squeeze.3.wanted, s32[2,64]{1,0:T(2,128)S(1)} %bitcast.38, f32[128,32,128]{2,1,0:T(8,128)S(1)} %copy-done.3, f32[32,32]{1,0:T(8,128)S(1)} %copy-done.20), custom_call_target="tpu_custom_call" | custom-call | tf_op jit(solution)/shard_map/pallas_call | solution.py:288
  100.3 1.0 copy-done.8
  101.2 0.8 copy-done.12
  102.0 22.6 %shard_map.63 = (bf16[16,4,32,128]{3,2,1,0:T(8,128)(2,1)}, bf16[2,64,32,128]{3,2,1,0:T(8,128)(2,1)}) custom-call(bf16[16,4,32,128]{3,2,1,0:T(8,128)(2,1)} %bitcast.28, bf16[2,64,32,128]{3,2,1,0:T(8,128)(2,1)} %copy-done.8), custom_call_target="tpu_custom_call" | custom-call | tf_op jit(solution)/shard_map/pallas_call | solution.py:70
  124.7 1.2 copy-done.4
  125.9 1.0 copy-done.18
  126.9 3.2 %shard_map.64 = (bf16[64,32,128]{2,1,0:T(8,128)(2,1)S(1)}, bf16[64,32,128]{2,1,0:T(8,128)(2,1)S(1)}) custom-call(s32[64]{0:T(128)S(1)} %get-tuple-element.49.perm, s32[64]{0:T(128)S(1)} %get-tuple-element.50.cols, s32[64]{0:T(128)S(1)} %compare_convert_fusion.live, bf16[64,128,128]{2,1,0:T(8,128)(2,1)S(1)} %copy-done, bf16[64,32,128]{2,1,0:T(8,128)(2,1)S(1)} %bitcast.34, ...), custom_call_target="tpu_custom_call" | custom-call | tf_op jit(solution)/shard_map/pallas_call | solution.py:302
  130.2 0.8 copy-done.14
  131.0 0.8 copy-done.15
  131.8 18.9 %shard_map.65 = (bf16[16,4,32,128]{3,2,1,0:T(8,128)(2,1)}, bf16[2,64,32,128]{3,2,1,0:T(8,128)(2,1)}) custom-call(bf16[16,4,32,128]{3,2,1,0:T(8,128)(2,1)} %bitcast.30, bf16[1,64,32,128]{3,2,1,0:T(8,128)(2,1)} %bitcast.31), custom_call_target="tpu_custom_call" | custom-call | tf_op jit(solution)/shard_map/pallas_call | solution.py:70
  150.7 1.2 copy-done.6
  151.9 1.0 copy-done.10
  152.9 6.0 %shard_map.66 = (f32[128,32,128]{2,1,0:T(8,128)S(1)}, f32[8,128]{1,0:T(8,128)S(1)}) custom-call(s32[64]{0:T(128)S(1)} %reshape_squeeze.3.wanted, s32[2,64]{1,0:T(2,128)S(1)} %bitcast.39, bf16[64,32,128]{2,1,0:T(8,128)(2,1)S(1)} %bitcast.26, bf16[2,64,32,128]{3,2,1,0:T(8,128)(2,1)S(1)} %copy-done.6), custom_call_target="tpu_custom_call" | custom-call | tf_op jit(solution)/shard_map/pallas_call | solution.py:312
  158.9 0.6 copy-done.22
  159.5 14.2 %shard_map.67.inverse = f32[32,32]{1,0:T(8,128)} custom-call(f32[8,128]{1,0:T(8,128)} %copy-done.22), custom_call_target="tpu_custom_call" | custom-call | tf_op jit(solution)/shard_map/pallas_call | solution.py:320
  173.7 0.7 copy-done.21
  174.4 2.6 %shard_map.68 = f32[32,16384]{1,0:T(8,128)} custom-call(f32[128,32,128]{2,1,0:T(8,128)S(1)} %get-tuple-element.47.source, f32[32,32]{1,0:T(8,128)S(1)} %copy-done.21), custom_call_target="tpu_custom_call" | custom-call | tf_op jit(solution)/shard_map/pallas_call | solution.py:336
  (27 shorter events, 0.1 us)
Async XLA Ops:
  0.0 43.2 %copy-start = (bf16[64,128,128]{2,1,0:T(8,128)(2,1)S(1)}, bf16[64,128,128]{2,1,0:T(8,128)(2,1)}, u32[]{:S(2)}) copy-start(bf16[64,128,128]{2,1,0:T(8,128)(2,1)} %blocks.3) | copy-start | bytes 6291460
  16.6 1.6 copy-start.1
  19.5 1.0 copy-start.9
  20.4 0.8 copy-start.13
  43.2 1.2 copy-start.5
  44.4 1.0 copy-start.19
  48.6 0.8 copy-start.16
  49.5 0.8 copy-start.17
  70.1 1.2 copy-start.7
  71.3 1.0 copy-start.11
  78.3 1.3 copy-start.2
  79.7 0.6 copy-start.23
  93.8 1.6 copy-start.3
  95.3 0.7 copy-start.20
  100.3 1.0 copy-start.8
  101.2 0.8 copy-start.12
  124.7 1.2 copy-start.4
  125.9 1.0 copy-start.18
  130.1 0.8 copy-start.14
  131.0 0.8 copy-start.15
  150.7 1.2 copy-start.6
  151.9 1.0 copy-start.10
  158.9 0.6 copy-start.22
  173.6 0.7 copy-start.21

commit v2 on v1

v2 whole, which is shorter than its diff:
```python
import functools

import jax
import jax.numpy as jnp
from jax import lax
from jax.experimental import pallas as pl
from jax.experimental.pallas import tpu as pltpu
from jax.sharding import PartitionSpec as P

ITERS = 2
MESH = pl.DeviceIdType.MESH
ANY = pl.BlockSpec(memory_space=pl.ANY)
VMEM = pl.BlockSpec(memory_space=pltpu.VMEM)
SMEM = pl.BlockSpec(memory_space=pltpu.SMEM)
VMEM_BYTES = 48 << 20


def greet(n_row, n_col):
    my_row, my_col = lax.axis_index("row"), lax.axis_index("col")
    barrier = pltpu.get_barrier_semaphore()
    for d in range(1, n_col):
        peer = lax.rem(my_col + d, n_col)
        pl.semaphore_signal(barrier, inc=1, device_id=(my_row, peer), device_id_type=MESH)
    for d in range(1, n_row):
        peer = lax.rem(my_row + d, n_row)
        pl.semaphore_signal(barrier, inc=1, device_id=(peer, my_col), device_id_type=MESH)
    pl.semaphore_wait(barrier, n_col + n_row - 2)
    return my_row, my_col


def exchange_kernel(n_row, n_col, c_src, r_src, c_dst, r_dst, own, c_send, c_recv, r_send, r_recv):
    my_row, my_col = greet(n_row, n_col)
    shared = r_src.shape[0] == 1
    copies = []
    for d in range(1, n_row):
        peer = lax.rem(my_row + d, n_row)
        copies.append(
            pltpu.make_async_remote_copy(
                src_ref=r_src.at[0 if shared else peer],
                dst_ref=r_dst.at[my_row],
                send_sem=r_send.at[d],
                recv_sem=r_recv.at[d],
                device_id=(peer, my_col),
                device_id_type=MESH,
            )
        )
    for d in range(1, n_col):
        peer = lax.rem(my_col + d, n_col)
        copies.append(
            pltpu.make_async_remote_copy(
                src_ref=c_src.at[peer],
                dst_ref=c_dst.at[my_col],
                send_sem=c_send.at[d],
                recv_sem=c_recv.at[d],
                device_id=(my_row, peer),
                device_id_type=MESH,
            )
        )
    copies.append(pltpu.make_async_copy(c_src.at[my_col], c_dst.at[my_col], own.at[0]))
    copies.append(
        pltpu.make_async_copy(r_src.at[0 if shared else my_row], r_dst.at[my_row], own.at[1])
    )
    for copy in copies:
        copy.start()
    for copy in copies:
        copy.wait()


def exchange(n_row, n_col, collective_id, c_src, r_src):
    return pl.pallas_call(
        functools.partial(exchange_kernel, n_row, n_col),
        out_shape=(
            jax.ShapeDtypeStruct(c_src.shape, c_src.dtype),
            jax.ShapeDtypeStruct((n_row,) + r_src.shape[1:], r_src.dtype),
        ),
        in_specs=[ANY, ANY],
        out_specs=(ANY, ANY),
        scratch_shapes=[
            pltpu.SemaphoreType.DMA((2,)),
            pltpu.SemaphoreType.DMA((n_col,)),
            pltpu.SemaphoreType.DMA((n_col,)),
            pltpu.SemaphoreType.DMA((n_row,)),
            pltpu.SemaphoreType.DMA((n_row,)),
        ],
        compiler_params=pltpu.CompilerParams(collective_id=collective_id, has_side_effects=True),
    )(c_src, r_src)


def split(value):
    high = value.astype(jnp.bfloat16)
    return high, (value - high.astype(jnp.float32)).astype(jnp.bfloat16)


def inverse_stack(inverse):
    high, low = split(inverse)
    return jnp.concatenate([high, low, high, low], axis=1)


def apply_inverse(stacked, product):
    high, low = split(product)
    parts = jnp.concatenate([high, high, low, low], axis=0)
    return jnp.dot(stacked, parts, preferred_element_type=jnp.float32)


def factor_inverse(packed, size):
    full = jnp.concatenate([packed[:, size * i : size * (i + 1)] for i in range(size // 8)], axis=0)
    rows = lax.broadcasted_iota(jnp.int32, (size, size), 0)
    lanes = lax.broadcasted_iota(jnp.int32, (size, size), 1)
    work = jnp.concatenate([full, (rows == lanes).astype(jnp.float32)], axis=1)
    row_ids = lax.broadcasted_iota(jnp.int32, (size, 2 * size), 0)
    for j in range(size):
        scale = 1.0 / jnp.sqrt(work[j : j + 1, j : j + 1])
        pivot_row = work[j : j + 1, :] * scale
        factors = work[:, j : j + 1] * scale
        work = jnp.where(
            row_ids > j, work - factors * pivot_row, jnp.where(row_ids == j, pivot_row, work)
        )
    return work[:, size:]


def sum_over_mesh(n_row, n_col, gram, row_in, row_sum, col_in, r_send, r_recv, c_send, c_recv):
    my_row, my_col = lax.axis_index("row"), lax.axis_index("col")
    copies = []
    for d in range(1, n_row):
        peer = lax.rem(my_row + d, n_row)
        copies.append(
            pltpu.make_async_remote_copy(
                src_ref=gram,
                dst_ref=row_in.at[my_row],
                send_sem=r_send.at[d],
                recv_sem=r_recv.at[d],
                device_id=(peer, my_col),
                device_id_type=MESH,
            )
        )
    for copy in copies:
        copy.start()
    row_in[my_row] = gram[...]
    for copy in copies:
        copy.wait()
    row_sum[...] = jnp.sum(row_in[...], axis=0)
    copies = []
    for d in range(1, n_col):
        peer = lax.rem(my_col + d, n_col)
        copies.append(
            pltpu.make_async_remote_copy(
                src_ref=row_sum,
                dst_ref=col_in.at[my_col],
                send_sem=c_send.at[d],
                recv_sem=c_recv.at[d],
                device_id=(my_row, peer),
                device_id_type=MESH,
            )
        )
    for copy in copies:
        copy.start()
    col_in[my_col] = row_sum[...]
    for copy in copies:
        copy.wait()
    return jnp.sum(col_in[...], axis=0)


def product_kernel(first, n_row, n_col, pieces, panel, order, *refs):
    if first:
        wanted, all_cols, perm, cols, live, source, blocks = refs[:7]
        refs = refs[7:]
    else:
        wanted, all_cols, perm, cols, live, product, gram, blocks = refs[:8]
        refs = refs[8:]
    row_terms, col_terms = refs[:2]
    held, c_out, c_in, c_back, r_out, r_in, r_back, held_blocks, own = refs[2:11]
    sems = refs[11:19]
    c_send, c_recv, r_send, r_recv, cb_send, cb_recv, rb_send, rb_recv = sems
    share = c_out.shape[1]
    per_piece = n_col // pieces
    my_row, my_col = lax.axis_index("row"), lax.axis_index("col")
    base = my_row * panel

    load_blocks = pltpu.make_async_copy(blocks, held_blocks, own.at[0])
    load_blocks.start()
    if first:
        for b in range(panel):
            held[b] = source[:, b * 128 : (b + 1) * 128].astype(jnp.bfloat16)
        greet(n_row, n_col)
    else:
        product_in = refs[19]
        load_product = pltpu.make_async_copy(product, product_in, own.at[1])
        load_product.start()
        greet(n_row, n_col)
        packed = sum_over_mesh(n_row, n_col, gram, *refs[20:]) / order
        stacked = inverse_stack(factor_inverse(packed, held.shape[1]))
        load_product.wait()

        def round_block(b, carry):
            held[b] = apply_inverse(stacked, product_in[b]).astype(jnp.bfloat16)
            return carry

        lax.fori_loop(0, panel, round_block, 0, unroll=8)

    c_copies, r_copies = [None] * n_col, []
    for j in range(pieces):
        for e in range(n_row):
            p = lax.rem(my_row + e, n_row)

            for d in range(j * per_piece, (j + 1) * per_piece):
                q = lax.rem(my_col + n_col - d, n_col)

                def one_r(a, carry):
                    at = jnp.clip(all_cols[p, q * share + a] - base, 0, panel - 1)
                    target = r_in if e == 0 else r_out
                    target[p, j, (d - j * per_piece) * share + a] = held[at]
                    return carry

                lax.fori_loop(0, share, one_r, 0, unroll=share)
            if e > 0:
                copy = pltpu.make_async_remote_copy(
                    src_ref=r_out.at[p, j],
                    dst_ref=r_in.at[my_row, j],
                    send_sem=r_send.at[e, j],
                    recv_sem=r_recv.at[e, j],
                    device_id=(p, my_col),
                    device_id_type=MESH,
                )
                copy.start()
                r_copies.append((j, copy))
        for d in range(j * per_piece, (j + 1) * per_piece):
            p = lax.rem(my_col + d, n_col)
            target = c_in if d == 0 else c_out

            def one_c(a, carry):
                target[p, a] = held[wanted[p * share + a]]
                return carry

            lax.fori_loop(0, share, one_c, 0, unroll=share)
            if d > 0:
                copy = pltpu.make_async_remote_copy(
                    src_ref=c_out.at[p],
                    dst_ref=c_in.at[my_col],
                    send_sem=c_send.at[d],
                    recv_sem=c_recv.at[d],
                    device_id=(my_row, p),
                    device_id_type=MESH,
                )
                copy.start()
                c_copies[d] = copy
    load_blocks.wait()

    back = []
    for j in range(pieces):
        for piece, copy in r_copies:
            if piece == j:
                copy.wait()
        for d in range(j * per_piece, (j + 1) * per_piece):
            q = lax.rem(my_col + n_col - d, n_col)
            if d > 0:
                c_copies[d].wait()

            def one_slot(a, carry):
                t = q * share + a
                at = (d - j * per_piece) * share + a
                block = held_blocks[perm[t]]
                alive = live[t] > 0
                x_col = r_in[0, j, at]
                for p in range(1, n_row):
                    x_col = jnp.where(cols[t] // panel == p, r_in[p, j, at], x_col)
                row_product = lax.dot_general(
                    x_col, block, (((1,), (1,)), ((), ())), preferred_element_type=jnp.float32
                )
                col_product = jnp.dot(c_in[q, a], block, preferred_element_type=jnp.float32)
                c_back[q, a] = jnp.where(alive, row_product, 0.0).astype(jnp.bfloat16)
                r_back[j, at] = jnp.where(alive, col_product, 0.0).astype(jnp.bfloat16)
                return carry

            lax.fori_loop(0, share, one_slot, 0, unroll=share)
            if d == 0:
                copy = pltpu.make_async_copy(c_back.at[q], row_terms.at[my_col], own.at[2])
            else:
                copy = pltpu.make_async_remote_copy(
                    src_ref=c_back.at[q],
                    dst_ref=row_terms.at[my_col],
                    send_sem=cb_send.at[d],
                    recv_sem=cb_recv.at[d],
                    device_id=(my_row, q),
                    device_id_type=MESH,
                )
            copy.start()
            back.append(copy)
        for e in range(n_row):
            p = lax.rem(my_row + e, n_row)
            if e == 0:
                copy = pltpu.make_async_copy(
                    r_back.at[j], col_terms.at[my_row, j], own.at[3 + j]
                )
            else:
                copy = pltpu.make_async_remote_copy(
                    src_ref=r_back.at[j],
                    dst_ref=col_terms.at[my_row, j],
                    send_sem=rb_send.at[e, j],
                    recv_sem=rb_recv.at[e, j],
                    device_id=(p, my_col),
                    device_id_type=MESH,
                )
            copy.start()
            back.append(copy)
    for copy in back:
        copy.wait()


def sum_kernel(
    n_col, wanted, all_cols, row_terms, col_terms, product, gram, row_held, col_held, sem
):
    panel, vectors = product.shape[0], product.shape[1]
    share = row_terms.shape[0] // n_col
    my_row, my_col = lax.axis_index("row"), lax.axis_index("col")
    base = my_row * panel
    load_rows = pltpu.make_async_copy(row_terms, row_held, sem.at[0])
    load_cols = pltpu.make_async_copy(col_terms, col_held, sem.at[1])
    load_rows.start()
    load_cols.start()
    product[...] = jnp.zeros_like(product)
    load_rows.wait()

    def one_row(t, carry):
        at = wanted[t]
        product[at] = product[at] + row_held[t].astype(jnp.float32)
        return carry

    lax.fori_loop(0, row_held.shape[0], one_row, 0, unroll=4)
    load_cols.wait()
    for p in range(all_cols.shape[0]):

        def one_col(i, carry):
            owner = lax.rem(my_col + n_col - i // share, n_col)
            at = all_cols[p, owner * share + lax.rem(i, share)] - base

            @pl.when((at >= 0) & (at < panel))
            def _():
                product[at] = product[at] + col_held[p, i].astype(jnp.float32)

            return carry

        lax.fori_loop(0, col_held.shape[1], one_col, 0, unroll=4)

    def one_gram(b, total):
        high, low = split(product[b])
        parts = jnp.concatenate([high, low], axis=0)
        return total + lax.dot_general(
            parts, parts, (((1,), (1,)), ((), ())), preferred_element_type=jnp.float32
        )

    total = lax.fori_loop(
        0, panel, one_gram, jnp.zeros((2 * vectors, 2 * vectors), jnp.float32), unroll=8
    )
    upper = total[:vectors] + total[vectors:]
    full = upper[:, :vectors] + upper[:, vectors:]
    gram[...] = jnp.concatenate([full[8 * i : 8 * i + 8] for i in range(vectors // 8)], axis=1)


def factor_kernel(n_row, n_col, order, gram, inverse, *scratch):
    greet(n_row, n_col)
    packed = sum_over_mesh(n_row, n_col, gram, *scratch) / order
    inverse[...] = factor_inverse(packed, inverse.shape[0])


def finish_kernel(source, inverse, out):
    stacked = inverse_stack(inverse[...])
    for b in range(source.shape[0]):
        out[:, b * 128 : (b + 1) * 128] = apply_inverse(stacked, source[b])


def local_params():
    return pltpu.CompilerParams(vmem_limit_bytes=VMEM_BYTES)


def per_device(n_row, n_col, blocks, block_rows, block_cols, counts, start_vectors):
    slots, size = blocks.shape[0], blocks.shape[1]
    vectors, width = start_vectors.shape
    panel = width // size
    share = slots // n_col
    bf16, f32 = jnp.bfloat16, jnp.float32
    shape = jax.ShapeDtypeStruct

    rows, cols, ids = block_rows[0], block_cols[0], jnp.arange(slots, dtype=jnp.int32)
    owner = rows // panel
    earlier = (owner[None, :] == owner[:, None]) & (ids[None, :] < ids[:, None])
    place = owner * share + jnp.sum(earlier.astype(jnp.int32), axis=1)
    here = (place[None, :] == ids[:, None]).astype(jnp.int32)
    perm = jnp.sum(here * ids[None, :], axis=1)
    rows = jnp.sum(here * rows[None, :], axis=1)
    cols = jnp.sum(here * cols[None, :], axis=1)
    live = (perm < counts[0, 0]).astype(jnp.int32)

    row_ask = jnp.pad((rows % panel).reshape(n_col, 1, share), ((0, 0), (0, 7), (0, 128 - share)))
    col_ask = jnp.pad(cols.reshape(1, 1, slots), ((0, 0), (0, 7), (0, 128 - slots)))
    row_got, col_got = exchange(n_row, n_col, 0, row_ask, col_ask)
    wanted = row_got[:, 0, :share].reshape(slots)
    all_cols = col_got[:, 0, :slots]

    gram_shape = (8, vectors * vectors // 8)
    pieces = 4 if n_col % 4 == 0 else 1
    dma = pltpu.SemaphoreType.DMA
    order = float(n_row * n_col * width)
    mesh_sum = [
        pltpu.VMEM((n_row,) + gram_shape, f32),
        pltpu.VMEM(gram_shape, f32),
        pltpu.VMEM((n_col,) + gram_shape, f32),
        dma((n_row,)),
        dma((n_row,)),
        dma((n_col,)),
        dma((n_col,)),
    ]
    by_owner = (n_col, share, vectors, size)
    by_piece = (pieces, slots // pieces, vectors, size)
    product = gram = None
    for iteration in range(ITERS):
        first = iteration == 0
        sources = (start_vectors,) if first else (product, gram)
        row_terms, col_terms = pl.pallas_call(
            functools.partial(product_kernel, first, n_row, n_col, pieces, panel, order),
            out_shape=(shape(by_owner, bf16), shape((n_row,) + by_piece, bf16)),
            in_specs=[SMEM] * 5 + ([VMEM] if first else [ANY, VMEM]) + [ANY],
            out_specs=(ANY, ANY),
            scratch_shapes=[
                pltpu.VMEM((panel, vectors, size), bf16),
                pltpu.VMEM(by_owner, bf16),
                pltpu.VMEM(by_owner, bf16),
                pltpu.VMEM(by_owner, bf16),
                pltpu.VMEM((n_row,) + by_piece, bf16),
                pltpu.VMEM((n_row,) + by_piece, bf16),
                pltpu.VMEM(by_piece, bf16),
                pltpu.VMEM(blocks.shape, bf16),
                dma((3 + pieces,)),
                dma((n_col,)),
                dma((n_col,)),
                dma((n_row, pieces)),
                dma((n_row, pieces)),
                dma((n_col,)),
                dma((n_col,)),
                dma((n_row, pieces)),
                dma((n_row, pieces)),
            ]
            + ([] if first else [pltpu.VMEM((panel, vectors, size), f32)] + mesh_sum),
            compiler_params=pltpu.CompilerParams(
                collective_id=1 if first else 2,
                has_side_effects=True,
                vmem_limit_bytes=VMEM_BYTES,
            ),
        )(wanted, all_cols, perm, cols, live, *sources, blocks)
        product, gram = pl.pallas_call(
            functools.partial(sum_kernel, n_col),
            out_shape=(shape((panel, vectors, size), f32), shape(gram_shape, f32)),
            in_specs=[SMEM, SMEM, ANY, ANY],
            out_specs=(VMEM, VMEM),
            scratch_shapes=[
                pltpu.VMEM((slots, vectors, size), bf16),
                pltpu.VMEM((n_row, slots, vectors, size), bf16),
                dma((2,)),
            ],
            compiler_params=local_params(),
        )(
            wanted,
            all_cols,
            row_terms.reshape(slots, vectors, size),
            col_terms.reshape(n_row, slots, vectors, size),
        )
    inverse = pl.pallas_call(
        functools.partial(factor_kernel, n_row, n_col, order),
        out_shape=shape((vectors, vectors), f32),
        in_specs=[VMEM],
        out_specs=VMEM,
        scratch_shapes=mesh_sum,
        compiler_params=pltpu.CompilerParams(collective_id=3, has_side_effects=True),
    )(gram)
    return pl.pallas_call(
        finish_kernel,
        out_shape=shape((vectors, width), f32),
        in_specs=[VMEM, VMEM],
        out_specs=VMEM,
        compiler_params=local_params(),
    )(product, inverse)


def solution(mesh):
    placed = (
        P("row", "col", None),
        P("row", "col"),
        P("row", "col"),
        P("row", "col"),
        P(None, ("row", "col")),
    )
    return jax.shard_map(
        functools.partial(per_device, mesh.shape["row"], mesh.shape["col"]),
        mesh=mesh,
        in_specs=placed,
        out_specs=P(None, ("row", "col")),
        check_vma=False,
    )
```

time: 178 us -> 131 us (0.74)
  Pallas kernels: 147 us -> 120 us
  local copies, waits for them, and re-layouts: 25.8 us -> 7.45 us
    pallas_call x5 -> x1, Pallas kernels: 93.1 us -> 9.79 us  [exchange(): pl.pallas_call(functools.partial(exchange_kernel, n_row, n_col), out_shap...]
    pallas_call x8 -> x5, Pallas kernels: 51.4 us -> 107 us  [the longest x2 78.4 us: per_device(): pl.pallas_call(functools.partial(product_kernel, first, n_row, n_col, pie...]
    unnamed x48 -> x10, local copies, waits for them, and re-layouts: 22.9 us -> 4.48 us
where the time goes in v2:
time: 131 us
  Pallas kernels  120 us (92%)
  local copies, waits for them, and re-layouts  7.45 us (6%)
  other arithmetic  3.04 us (2%)
    pallas_call x2, Pallas kernels, per_device(): pl.pallas_call(functools.partial(product_kernel, first, n_row, n_col, pie...  78.4 us
    pallas_call x2, Pallas kernels, per_device(): pl.pallas_call(functools.partial(sum_kernel, n_col), out_shape=(shape((pa...  14.8 us
    pallas_call x1, Pallas kernels, per_device(): pl.pallas_call(functools.partial(factor_kernel, n_row, n_col, order), out...  14.2 us
    pallas_call x1, Pallas kernels, exchange(): pl.pallas_call(functools.partial(exchange_kernel, n_row, n_col), out_shap...  9.79 us
    unnamed x10, local copies, waits for them, and re-layouts  4.48 us

profile of v2, /device:TPU:0, one launch (start us, length us, event | category | flops | bytes accessed | tf_op | source)
XLA Modules:
  0.0 131.0 jit_solution(10439999746646050112)
XLA Ops:
  0.7 0.7 and_select_fusion.1
  1.3 0.7 fusion.3
  2.0 0.2 convert_reduce_fusion
  2.2 0.7 fusion.2
  2.8 0.8 select_reduce_fusion
  3.7 0.6 pad.9.r_src
  4.3 0.1 reduce_sum.43
  4.4 0.6 pad.8.c_src
  5.0 9.8 %shard_map.55 = (s32[16,8,128]{2,1,0:T(8,128)}, s32[2,8,128]{2,1,0:T(8,128)}) custom-call(s32[16,8,128]{2,1,0:T(8,128)} %pad.8.c_src, s32[1,8,128]{2,1,0:T(8,128)} %pad.9.r_src), custom_call_target="tpu_custom_call" | custom-call | tf_op jit(solution)/shard_map/pallas_call | solution.py:70
  14.8 0.9 slice_reduce_fusion
  15.7 0.1 reshape_squeeze.3.refs_0_.wanted
  15.8 0.7 slice.7
  16.5 0.0 copy-start
  16.5 1.6 %copy-done = bf16[64,128,128]{2,1,0:T(8,128)(2,1)S(1)} copy-done((bf16[64,128,128]{2,1,0:T(8,128)(2,1)S(1)}, bf16[64,128,128]{2,1,0:T(8,128)(2,1)}, u32[]{:S(2)}) %copy-start) | copy-done | bytes 2097176
  18.1 0.0 copy-start.2
  18.1 1.6 %copy-done.2 = f32[32,16384]{1,0:T(8,128)S(1)} copy-done((f32[32,16384]{1,0:T(8,128)S(1)}, f32[32,16384]{1,0:T(8,128)}, u32[]{:S(2)}) %copy-start.2) | copy-done | bytes 2097176
  19.7 0.0 copy-start.1
  19.7 32.6 %shard_map.56 = (bf16[16,4,32,128]{3,2,1,0:T(8,128)(2,1)S(1)}, bf16[2,4,16,32,128]{4,3,2,1,0:T(8,128)(2,1)S(1)}) custom-call(s32[64]{0:T(128)S(1)} %reshape_squeeze.3.refs_0_.wanted, s32[2,64]{1,0:T(2,128)S(1)} %bitcast.24, s32[64]{0:T(128)S(1)} %get-tuple-element.25.refs_2_, s32[64]{0:T(128)S(1)} %get-tuple-element.26.refs_3_, ...), custom_call_target="tpu_custom_call" | custom-call | tf_op jit(solution)/shard_map/pallas_call | solution.py:418
  52.3 7.4 %shard_map.57 = (f32[128,32,128]{2,1,0:T(8,128)S(1)}, f32[8,128]{1,0:T(8,128)S(1)}) custom-call(s32[64]{0:T(128)S(1)} %reshape_squeeze.3.refs_0_.wanted, s32[2,64]{1,0:T(2,128)S(1)} %bitcast.25, bf16[64,32,128]{2,1,0:T(8,128)(2,1)S(1)} %bitcast.23, bf16[2,64,32,128]{3,2,1,0:T(8,128)(2,1)S(1)} %bitcast.21), custom_call_target="tpu_custom_call" | custom-call | tf_op jit(solution)/shard_map/pallas_call | solution.py:449
  59.7 0.0 copy-done.1
  59.7 45.7 %shard_map.58 = (bf16[16,4,32,128]{3,2,1,0:T(8,128)(2,1)S(1)}, bf16[2,4,16,32,128]{4,3,2,1,0:T(8,128)(2,1)S(1)}) custom-call(s32[64]{0:T(128)S(1)} %reshape_squeeze.3.refs_0_.wanted, s32[2,64]{1,0:T(2,128)S(1)} %bitcast.26, s32[64]{0:T(128)S(1)} %get-tuple-element.25.refs_2_, s32[64]{0:T(128)S(1)} %get-tuple-element.26.refs_3_, ...), custom_call_target="tpu_custom_call" | custom-call | tf_op jit(solution)/shard_map/pallas_call | solution.py:418
  105.4 7.4 %shard_map.59 = (f32[128,32,128]{2,1,0:T(8,128)S(1)}, f32[8,128]{1,0:T(8,128)S(1)}) custom-call(s32[64]{0:T(128)S(1)} %reshape_squeeze.3.refs_0_.wanted, s32[2,64]{1,0:T(2,128)S(1)} %bitcast.27, bf16[64,32,128]{2,1,0:T(8,128)(2,1)S(1)} %bitcast.22, bf16[2,64,32,128]{3,2,1,0:T(8,128)(2,1)S(1)} %bitcast.20), custom_call_target="tpu_custom_call" | custom-call | tf_op jit(solution)/shard_map/pallas_call | solution.py:449
  112.8 0.0 copy-start.4
  112.8 0.6 copy-done.4
  113.4 14.2 %shard_map.60.inverse = f32[32,32]{1,0:T(8,128)} custom-call(f32[8,128]{1,0:T(8,128)} %copy-done.4), custom_call_target="tpu_custom_call" | custom-call | tf_op jit(solution)/shard_map/pallas_call | solution.py:466
  127.7 0.0 copy-start.3
  127.7 0.7 copy-done.3
  128.4 2.6 %shard_map.61 = f32[32,16384]{1,0:T(8,128)} custom-call(f32[128,32,128]{2,1,0:T(8,128)S(1)} %get-tuple-element.23.source, f32[32,32]{1,0:T(8,128)S(1)} %copy-done.3), custom_call_target="tpu_custom_call" | custom-call | tf_op jit(solution)/shard_map/pallas_call | solution.py:474
  (2 shorter events, 0.0 us)
Async XLA Ops:
  16.5 1.6 %copy-start = (bf16[64,128,128]{2,1,0:T(8,128)(2,1)S(1)}, bf16[64,128,128]{2,1,0:T(8,128)(2,1)}, u32[]{:S(2)}) copy-start(bf16[64,128,128]{2,1,0:T(8,128)(2,1)} %refs_7_.1) | copy-start | bytes 6291460
  18.1 1.6 %copy-start.2 = (f32[32,16384]{1,0:T(8,128)S(1)}, f32[32,16384]{1,0:T(8,128)}, u32[]{:S(2)}) copy-start(f32[32,16384]{1,0:T(8,128)} %refs_5_.1) | copy-start | bytes 6291460
  19.7 40.0 %copy-start.1 = (bf16[64,128,128]{2,1,0:T(8,128)(2,1)S(1)}, bf16[64,128,128]{2,1,0:T(8,128)(2,1)}, u32[]{:S(2)}) copy-start(bf16[64,128,128]{2,1,0:T(8,128)(2,1)} %refs_7_.1) | copy-start | bytes 6291460
  112.8 0.6 copy-start.4
  127.7 0.7 copy-start.3

commit v3 on v2

--- a/solution.py
+++ b/solution.py
@@ -9,7 +9,7 @@
 
 ITERS = 2
 MESH = pl.DeviceIdType.MESH
-ANY = pl.BlockSpec(memory_space=pl.ANY)
+HBM = pl.BlockSpec(memory_space=pltpu.HBM)
 VMEM = pl.BlockSpec(memory_space=pltpu.VMEM)
 SMEM = pl.BlockSpec(memory_space=pltpu.SMEM)
 VMEM_BYTES = 48 << 20
@@ -28,64 +28,6 @@
     return my_row, my_col
 
 
-def exchange_kernel(n_row, n_col, c_src, r_src, c_dst, r_dst, own, c_send, c_recv, r_send, r_recv):
-    my_row, my_col = greet(n_row, n_col)
-    shared = r_src.shape[0] == 1
-    copies = []
-    for d in range(1, n_row):
-        peer = lax.rem(my_row + d, n_row)
-        copies.append(
-            pltpu.make_async_remote_copy(
-                src_ref=r_src.at[0 if shared else peer],
-                dst_ref=r_dst.at[my_row],
-                send_sem=r_send.at[d],
-                recv_sem=r_recv.at[d],
-                device_id=(peer, my_col),
-                device_id_type=MESH,
-            )
-        )
-    for d in range(1, n_col):
-        peer = lax.rem(my_col + d, n_col)
-        copies.append(
-            pltpu.make_async_remote_copy(
-                src_ref=c_src.at[peer],
-                dst_ref=c_dst.at[my_col],
-                send_sem=c_send.at[d],
-                recv_sem=c_recv.at[d],
-                device_id=(my_row, peer),
-                device_id_type=MESH,
-            )
-        )
-    copies.append(pltpu.make_async_copy(c_src.at[my_col], c_dst.at[my_col], own.at[0]))
-    copies.append(
-        pltpu.make_async_copy(r_src.at[0 if shared else my_row], r_dst.at[my_row], own.at[1])
-    )
-    for copy in copies:
-        copy.start()
-    for copy in copies:
-        copy.wait()
-
-
-def exchange(n_row, n_col, collective_id, c_src, r_src):
-    return pl.pallas_call(
-        functools.partial(exchange_kernel, n_row, n_col),
-        out_shape=(
-            jax.ShapeDtypeStruct(c_src.shape, c_src.dtype),
-            jax.ShapeDtypeStruct((n_row,) + r_src.shape[1:], r_src.dtype),
-        ),
-        in_specs=[ANY, ANY],
-        out_specs=(ANY, ANY),
-        scratch_shapes=[
-            pltpu.SemaphoreType.DMA((2,)),
-            pltpu.SemaphoreType.DMA((n_col,)),
-            pltpu.SemaphoreType.DMA((n_col,)),
-            pltpu.SemaphoreType.DMA((n_row,)),
-            pltpu.SemaphoreType.DMA((n_row,)),
-        ],
-        compiler_params=pltpu.CompilerParams(collective_id=collective_id, has_side_effects=True),
-    )(c_src, r_src)
-
-
 def split(value):
     high = value.astype(jnp.bfloat16)
     return high, (value - high.astype(jnp.float32)).astype(jnp.bfloat16)
@@ -94,6 +36,10 @@
 def inverse_stack(inverse):
     high, low = split(inverse)
     return jnp.concatenate([high, low, high, low], axis=1)
+
+
+def pair(blocks, i):
+    return jnp.concatenate([blocks[2 * i], blocks[2 * i + 1]], axis=1)
 
 
 def apply_inverse(stacked, product):
@@ -107,15 +53,12 @@
     rows = lax.broadcasted_iota(jnp.int32, (size, size), 0)
     lanes = lax.broadcasted_iota(jnp.int32, (size, size), 1)
     work = jnp.concatenate([full, (rows == lanes).astype(jnp.float32)], axis=1)
-    row_ids = lax.broadcasted_iota(jnp.int32, (size, 2 * size), 0)
+    row_ids = lax.broadcasted_iota(jnp.int32, (size, 1), 0)
     for j in range(size):
-        scale = 1.0 / jnp.sqrt(work[j : j + 1, j : j + 1])
-        pivot_row = work[j : j + 1, :] * scale
-        factors = work[:, j : j + 1] * scale
-        work = jnp.where(
-            row_ids > j, work - factors * pivot_row, jnp.where(row_ids == j, pivot_row, work)
-        )
-    return work[:, size:]
+        factors = work[:, j : j + 1] * (1.0 / work[j : j + 1, j : j + 1])
+        work = work - jnp.where(row_ids > j, factors, 0.0) * work[j : j + 1, :]
+    pivots = jnp.sum(jnp.where(rows == lanes, work[:, :size], 0.0), axis=1, keepdims=True)
+    return work[:, size:] * (1.0 / jnp.sqrt(pivots))
 
 
 def sum_over_mesh(n_row, n_col, gram, row_in, row_sum, col_in, r_send, r_recv, c_send, c_recv):
@@ -162,8 +105,9 @@
 
 def product_kernel(first, n_row, n_col, pieces, panel, order, *refs):
     if first:
-        wanted, all_cols, perm, cols, live, source, blocks = refs[:7]
-        refs = refs[7:]
+        row_ask, col_ask, perm, cols, live, source, blocks = refs[:7]
+        wanted_out, all_cols_out = refs[7:9]
+        refs = refs[9:]
     else:
         wanted, all_cols, perm, cols, live, product, gram, blocks = refs[:8]
         refs = refs[8:]
@@ -179,9 +123,53 @@
     load_blocks = pltpu.make_async_copy(blocks, held_blocks, own.at[0])
     load_blocks.start()
     if first:
+        source_in, wanted, all_cols, asked, ac_send, ac_recv, ar_send, ar_recv = refs[19:]
+        load_source = pltpu.make_async_copy(source, source_in, own.at[1])
+        load_source.start()
+        greet(n_row, n_col)
+        asks = [
+            pltpu.make_async_copy(row_ask.at[my_col], wanted_out.at[my_col], asked.at[0]),
+            pltpu.make_async_copy(col_ask.at[0], all_cols_out.at[my_row], asked.at[1]),
+        ]
+        for d in range(1, n_row):
+            peer = lax.rem(my_row + d, n_row)
+            asks.append(
+                pltpu.make_async_remote_copy(
+                    src_ref=col_ask.at[0],
+                    dst_ref=all_cols_out.at[my_row],
+                    send_sem=ar_send.at[d],
+                    recv_sem=ar_recv.at[d],
+                    device_id=(peer, my_col),
+                    device_id_type=MESH,
+                )
+            )
+        for d in range(1, n_col):
+            peer = lax.rem(my_col + d, n_col)
+            asks.append(
+                pltpu.make_async_remote_copy(
+                    src_ref=row_ask.at[peer],
+                    dst_ref=wanted_out.at[my_col],
+                    send_sem=ac_send.at[d],
+                    recv_sem=ac_recv.at[d],
+                    device_id=(my_row, peer),
+                    device_id_type=MESH,
+                )
+            )
+        for copy in asks:
+            copy.start()
+        load_source.wait()
         for b in range(panel):
-            held[b] = source[:, b * 128 : (b + 1) * 128].astype(jnp.bfloat16)
-        greet(n_row, n_col)
+            held[b] = source_in[:, b * 128 : (b + 1) * 128].astype(jnp.bfloat16)
+        for copy in asks:
+            copy.wait()
+        lists = [
+            pltpu.make_async_copy(wanted_out, wanted, asked.at[2]),
+            pltpu.make_async_copy(all_cols_out, all_cols, asked.at[3]),
+        ]
+        for copy in lists:
+            copy.start()
+        for copy in lists:
+            copy.wait()
     else:
         product_in = refs[19]
         load_product = pltpu.make_async_copy(product, product_in, own.at[1])
@@ -191,11 +179,13 @@
         stacked = inverse_stack(factor_inverse(packed, held.shape[1]))
         load_product.wait()
 
-        def round_block(b, carry):
-            held[b] = apply_inverse(stacked, product_in[b]).astype(jnp.bfloat16)
+        def round_blocks(i, carry):
+            both = apply_inverse(stacked, pair(product_in, i)).astype(jnp.bfloat16)
+            held[2 * i] = both[:, :128]
+            held[2 * i + 1] = both[:, 128:]
             return carry
 
-        lax.fori_loop(0, panel, round_block, 0, unroll=8)
+        lax.fori_loop(0, panel // 2, round_blocks, 0, unroll=8)
 
     c_copies, r_copies = [None] * n_col, []
     for j in range(pieces):
@@ -206,7 +196,7 @@
                 q = lax.rem(my_col + n_col - d, n_col)
 
                 def one_r(a, carry):
-                    at = jnp.clip(all_cols[p, q * share + a] - base, 0, panel - 1)
+                    at = jnp.clip(all_cols[p, 0, q * share + a] - base, 0, panel - 1)
                     target = r_in if e == 0 else r_out
                     target[p, j, (d - j * per_piece) * share + a] = held[at]
                     return carry
@@ -228,7 +218,7 @@
             target = c_in if d == 0 else c_out
 
             def one_c(a, carry):
-                target[p, a] = held[wanted[p * share + a]]
+                target[p, a] = held[wanted[p, 0, a]]
                 return carry
 
             lax.fori_loop(0, share, one_c, 0, unroll=share)
@@ -320,36 +310,37 @@
     product[...] = jnp.zeros_like(product)
     load_rows.wait()
 
-    def one_row(t, carry):
-        at = wanted[t]
-        product[at] = product[at] + row_held[t].astype(jnp.float32)
+    def one_owner(q, carry):
+        for a in range(share):
+            at = wanted[q, 0, a]
+            product[at] = product[at] + row_held[q * share + a].astype(jnp.float32)
         return carry
 
-    lax.fori_loop(0, row_held.shape[0], one_row, 0, unroll=4)
+    lax.fori_loop(0, n_col, one_owner, 0, unroll=2)
     load_cols.wait()
     for p in range(all_cols.shape[0]):
 
-        def one_col(i, carry):
-            owner = lax.rem(my_col + n_col - i // share, n_col)
-            at = all_cols[p, owner * share + lax.rem(i, share)] - base
-
-            @pl.when((at >= 0) & (at < panel))
-            def _():
-                product[at] = product[at] + col_held[p, i].astype(jnp.float32)
-
+        def one_piece(d, carry):
+            owner = lax.rem(my_col + n_col - d, n_col)
+            for a in range(share):
+                at = all_cols[p, 0, owner * share + a] - base
+                term = col_held[p, d * share + a].astype(jnp.float32)
+                term = jnp.where((at >= 0) & (at < panel), term, 0.0)
+                at = jnp.clip(at, 0, panel - 1)
+                product[at] = product[at] + term
             return carry
 
-        lax.fori_loop(0, col_held.shape[1], one_col, 0, unroll=4)
-
-    def one_gram(b, total):
-        high, low = split(product[b])
+        lax.fori_loop(0, n_col, one_piece, 0, unroll=2)
+
+    def one_gram(i, total):
+        high, low = split(pair(product, i))
         parts = jnp.concatenate([high, low], axis=0)
         return total + lax.dot_general(
             parts, parts, (((1,), (1,)), ((), ())), preferred_element_type=jnp.float32
         )
 
     total = lax.fori_loop(
-        0, panel, one_gram, jnp.zeros((2 * vectors, 2 * vectors), jnp.float32), unroll=8
+        0, panel // 2, one_gram, jnp.zeros((2 * vectors, 2 * vectors), jnp.float32), unroll=8
     )
     upper = total[:vectors] + total[vectors:]
     full = upper[:, :vectors] + upper[:, vectors:]
@@ -364,8 +355,8 @@
 
 def finish_kernel(source, inverse, out):
     stacked = inverse_stack(inverse[...])
-    for b in range(source.shape[0]):
-        out[:, b * 128 : (b + 1) * 128] = apply_inverse(stacked, source[b])
+    for i in range(source.shape[0] // 2):
+        out[:, i * 256 : (i + 1) * 256] = apply_inverse(stacked, pair(source, i))
 
 
 def local_params():
@@ -390,12 +381,8 @@
     cols = jnp.sum(here * cols[None, :], axis=1)
     live = (perm < counts[0, 0]).astype(jnp.int32)
 
-    row_ask = jnp.pad((rows % panel).reshape(n_col, 1, share), ((0, 0), (0, 7), (0, 128 - share)))
-    col_ask = jnp.pad(cols.reshape(1, 1, slots), ((0, 0), (0, 7), (0, 128 - slots)))
-    row_got, col_got = exchange(n_row, n_col, 0, row_ask, col_ask)
-    wanted = row_got[:, 0, :share].reshape(slots)
-    all_cols = col_got[:, 0, :slots]
-
+    row_ask = jnp.pad((rows % panel).reshape(n_col, 1, share), ((0, 0), (0, 0), (0, 128 - share)))
+    col_ask = jnp.pad(cols.reshape(1, 1, slots), ((0, 0), (0, 0), (0, 128 - slots)))
     gram_shape = (8, vectors * vectors // 8)
     pieces = 4 if n_col % 4 == 0 else 1
     dma = pltpu.SemaphoreType.DMA
@@ -414,12 +401,19 @@
     product = gram = None
     for iteration in range(ITERS):
         first = iteration == 0
-        sources = (start_vectors,) if first else (product, gram)
-        row_terms, col_terms = pl.pallas_call(
+        if first:
+            lists, sources = (row_ask, col_ask), (start_vectors,)
+            list_shapes = (shape((n_col, 1, 128), jnp.int32), shape((n_row, 1, 128), jnp.int32))
+        else:
+            lists, sources, list_shapes = (wanted, all_cols), (product, gram), ()
+        *got, row_terms, col_terms = pl.pallas_call(
             functools.partial(product_kernel, first, n_row, n_col, pieces, panel, order),
-            out_shape=(shape(by_owner, bf16), shape((n_row,) + by_piece, bf16)),
-            in_specs=[SMEM] * 5 + ([VMEM] if first else [ANY, VMEM]) + [ANY],
-            out_specs=(ANY, ANY),
+            out_shape=list_shapes + (shape(by_owner, bf16), shape((n_row,) + by_piece, bf16)),
+            in_specs=([HBM] if first else [SMEM]) * 2
+            + [SMEM] * 3
+            + ([HBM] if first else [HBM, VMEM])
+            + [HBM],
+            out_specs=(HBM,) * (len(list_shapes) + 2),
             scratch_shapes=[
                 pltpu.VMEM((panel, vectors, size), bf16),
                 pltpu.VMEM(by_owner, bf16),
@@ -439,17 +433,32 @@
                 dma((n_row, pieces)),
                 dma((n_row, pieces)),
             ]
-            + ([] if first else [pltpu.VMEM((panel, vectors, size), f32)] + mesh_sum),
+            + (
+                [
+                    pltpu.VMEM((vectors, width), f32),
+                    pltpu.SMEM((n_col, 1, 128), jnp.int32),
+                    pltpu.SMEM((n_row, 1, 128), jnp.int32),
+                    dma((4,)),
+                    dma((n_col,)),
+                    dma((n_col,)),
+                    dma((n_row,)),
+                    dma((n_row,)),
+                ]
+                if first
+                else [pltpu.VMEM((panel, vectors, size), f32)] + mesh_sum
+            ),
             compiler_params=pltpu.CompilerParams(
                 collective_id=1 if first else 2,
                 has_side_effects=True,
                 vmem_limit_bytes=VMEM_BYTES,
             ),
-        )(wanted, all_cols, perm, cols, live, *sources, blocks)
+        )(*lists, perm, cols, live, *sources, blocks)
+        if first:
+            wanted, all_cols = got
         product, gram = pl.pallas_call(
             functools.partial(sum_kernel, n_col),
             out_shape=(shape((panel, vectors, size), f32), shape(gram_shape, f32)),
-            in_specs=[SMEM, SMEM, ANY, ANY],
+            in_specs=[SMEM, SMEM, HBM, HBM],
             out_specs=(VMEM, VMEM),
             scratch_shapes=[
                 pltpu.VMEM((slots, vectors, size), bf16),

time: 131 us -> 117 us (0.89)
  Pallas kernels: 120 us -> 108 us
  local copies, waits for them, and re-layouts: 7.45 us -> 4.57 us
    pallas_call x1 -> x0, Pallas kernels: 9.79 us -> none  [exchange(): pl.pallas_call(functools.partial(exchange_kernel, n_row, n_col), out_shap...]
    pallas_call x2, Pallas kernels: 14.8 us -> 7.91 us  [per_device(): pl.pallas_call(functools.partial(sum_kernel, n_col), out_shape=(shape((pa...]
    pallas_call x2, Pallas kernels: 78.4 us -> 84.4 us  [per_device(): pl.pallas_call(functools.partial(product_kernel, first, n_row, n_col, pie...]
    slice x2 -> x0, local copies, waits for them, and re-layouts: 1.57 us -> none  [the longest x1 0.86 us: per_device(): wanted = row_got[:, 0, :share].reshape(slots)]
where the time goes in v3:
time: 117 us
  Pallas kernels  108 us (92%)
  local copies, waits for them, and re-layouts  4.57 us (4%)
  other arithmetic  3.04 us (3%)
    pallas_call x2, Pallas kernels, per_device(): pl.pallas_call(functools.partial(product_kernel, first, n_row, n_col, pie...  84.4 us
    pallas_call x1, Pallas kernels, per_device(): pl.pallas_call(functools.partial(factor_kernel, n_row, n_col, order), out...  13.8 us
    pallas_call x2, Pallas kernels, per_device(): pl.pallas_call(functools.partial(sum_kernel, n_col), out_shape=(shape((pa...  7.91 us
    unnamed x10, local copies, waits for them, and re-layouts  4.48 us

profile of v3, /device:TPU:0, one launch (start us, length us, event | category | flops | bytes accessed | tf_op | source)
XLA Modules:
  0.0 116.6 jit_solution(10803540836041532479)
XLA Ops:
  0.7 0.7 and_select_fusion.1
  1.3 0.7 fusion.3
  2.0 0.2 convert_reduce_fusion
  2.2 0.7 fusion.2
  2.8 0.8 select_reduce_fusion
  3.7 0.1 reduce_sum.43
  3.8 0.0 copy-start
  3.8 1.6 %copy-done = bf16[64,128,128]{2,1,0:T(8,128)(2,1)S(1)} copy-done((bf16[64,128,128]{2,1,0:T(8,128)(2,1)S(1)}, bf16[64,128,128]{2,1,0:T(8,128)(2,1)}, u32[]{:S(2)}) %copy-start) | copy-done | bytes 2097176
  5.4 0.0 copy-start.2
  5.4 1.6 %copy-done.2 = f32[32,16384]{1,0:T(8,128)S(1)} copy-done((f32[32,16384]{1,0:T(8,128)S(1)}, f32[32,16384]{1,0:T(8,128)}, u32[]{:S(2)}) %copy-start.2) | copy-done | bytes 2097176
  7.0 0.0 copy-start.1
  7.0 39.5 %shard_map.55 = (s32[16,1,128]{2,1,0:T(1,128)S(1)}, s32[2,1,128]{2,1,0:T(1,128)S(1)}, bf16[16,4,32,128]{3,2,1,0:T(8,128)(2,1)S(1)}, bf16[2,4,16,32,128]{4,3,2,1,0:T(8,128)(2,1)S(1)}) custom-call(s32[16,1,128]{2,1,0:T(1,128)S(1)} %pad.8.refs_0_, s32[1,1,128]{2,1,0:T(1,128)S(1)} %pad.9.refs_1_, s32[64]{0:T(128)S(1)} %get-tuple-element.25.refs_2_, ...), custom_call_target="tpu_custom_call" | custom-call | tf_op jit(solution)/shard_map/pallas_call | solution.py:409
  46.5 4.0 %shard_map.56 = (f32[128,32,128]{2,1,0:T(8,128)S(1)}, f32[8,128]{1,0:T(8,128)S(1)}) custom-call(s32[16,1,128]{2,1,0:T(1,128)S(1)} %get-tuple-element.15.wanted.refs_0_, s32[2,1,128]{2,1,0:T(1,128)S(1)} %get-tuple-element.16.all_cols.refs_1_, bf16[64,32,128]{2,1,0:T(8,128)(2,1)S(1)} %bitcast.22, bf16[2,64,32,128]{3,2,1,0:T(8,128)(2,1)S(1)} %bitcast.20), custom_call_target="tpu_custom_call" | custom-call | tf_op jit(solution)/shard_map/pallas_call | solution.py:458
  50.5 0.0 copy-done.1
  50.5 44.9 %shard_map.57 = (bf16[16,4,32,128]{3,2,1,0:T(8,128)(2,1)S(1)}, bf16[2,4,16,32,128]{4,3,2,1,0:T(8,128)(2,1)S(1)}) custom-call(s32[16,1,128]{2,1,0:T(1,128)S(1)} %get-tuple-element.15.wanted.refs_0_, s32[2,1,128]{2,1,0:T(1,128)S(1)} %get-tuple-element.16.all_cols.refs_1_, s32[64]{0:T(128)S(1)} %get-tuple-element.25.refs_2_, s32[64]{0:T(128)S(1)} %get-tuple-element.26.refs_3_, ...), custom_call_target="tpu_custom_call" | custom-call | tf_op jit(solution)/shard_map/pallas_call | solution.py:409
  95.4 4.0 %shard_map.58 = (f32[128,32,128]{2,1,0:T(8,128)S(1)}, f32[8,128]{1,0:T(8,128)S(1)}) custom-call(s32[16,1,128]{2,1,0:T(1,128)S(1)} %get-tuple-element.15.wanted.refs_0_, s32[2,1,128]{2,1,0:T(1,128)S(1)} %get-tuple-element.16.all_cols.refs_1_, bf16[64,32,128]{2,1,0:T(8,128)(2,1)S(1)} %bitcast.21, bf16[2,64,32,128]{3,2,1,0:T(8,128)(2,1)S(1)} %bitcast.19), custom_call_target="tpu_custom_call" | custom-call | tf_op jit(solution)/shard_map/pallas_call | solution.py:458
  99.4 0.0 copy-start.4
  99.4 0.6 copy-done.4
  100.0 13.8 %shard_map.59.inverse = f32[32,32]{1,0:T(8,128)} custom-call(f32[8,128]{1,0:T(8,128)} %copy-done.4), custom_call_target="tpu_custom_call" | custom-call | tf_op jit(solution)/shard_map/pallas_call | solution.py:475
  113.8 0.0 copy-start.3
  113.8 0.7 copy-done.3
  114.5 2.1 %shard_map.60 = f32[32,16384]{1,0:T(8,128)} custom-call(f32[128,32,128]{2,1,0:T(8,128)S(1)} %get-tuple-element.23.source, f32[32,32]{1,0:T(8,128)S(1)} %copy-done.3), custom_call_target="tpu_custom_call" | custom-call | tf_op jit(solution)/shard_map/pallas_call | solution.py:483
  (4 shorter events, 0.1 us)
Async XLA Ops:
  3.8 1.6 %copy-start = (bf16[64,128,128]{2,1,0:T(8,128)(2,1)S(1)}, bf16[64,128,128]{2,1,0:T(8,128)(2,1)}, u32[]{:S(2)}) copy-start(bf16[64,128,128]{2,1,0:T(8,128)(2,1)} %refs_7_.1) | copy-start | bytes 6291460
  5.4 1.6 %copy-start.2 = (f32[32,16384]{1,0:T(8,128)S(1)}, f32[32,16384]{1,0:T(8,128)}, u32[]{:S(2)}) copy-start(f32[32,16384]{1,0:T(8,128)} %refs_5_.1) | copy-start | bytes 6291460
  7.0 43.5 %copy-start.1 = (bf16[64,128,128]{2,1,0:T(8,128)(2,1)S(1)}, bf16[64,128,128]{2,1,0:T(8,128)(2,1)}, u32[]{:S(2)}) copy-start(bf16[64,128,128]{2,1,0:T(8,128)(2,1)} %refs_7_.1) | copy-start | bytes 6291460
  99.4 0.6 copy-start.4
  113.8 0.7 copy-start.3

commit v4 on v3

--- a/solution.py
+++ b/solution.py
@@ -53,10 +53,11 @@
     rows = lax.broadcasted_iota(jnp.int32, (size, size), 0)
     lanes = lax.broadcasted_iota(jnp.int32, (size, size), 1)
     work = jnp.concatenate([full, (rows == lanes).astype(jnp.float32)], axis=1)
-    row_ids = lax.broadcasted_iota(jnp.int32, (size, 1), 0)
+    row_ids = lax.broadcasted_iota(jnp.int32, work.shape, 0)
     for j in range(size):
-        factors = work[:, j : j + 1] * (1.0 / work[j : j + 1, j : j + 1])
-        work = work - jnp.where(row_ids > j, factors, 0.0) * work[j : j + 1, :]
+        column = jnp.broadcast_to(work[:, j : j + 1], work.shape)
+        pivot_row = work[j : j + 1, :] * (1.0 / column[j : j + 1, :])
+        work = work - jnp.where(row_ids > j, column, 0.0) * pivot_row
     pivots = jnp.sum(jnp.where(rows == lanes, work[:, :size], 0.0), axis=1, keepdims=True)
     return work[:, size:] * (1.0 / jnp.sqrt(pivots))
 
@@ -478,7 +479,9 @@
         in_specs=[VMEM],
         out_specs=VMEM,
         scratch_shapes=mesh_sum,
-        compiler_params=pltpu.CompilerParams(collective_id=3, has_side_effects=True),
+        compiler_params=pltpu.CompilerParams(
+            collective_id=3, has_side_effects=True, vmem_limit_bytes=VMEM_BYTES
+        ),
     )(gram)
     return pl.pallas_call(
         finish_kernel,

time: 117 us -> 114 us (0.974)
  local copies, waits for them, and re-layouts: 4.57 us -> 3.28 us
    unnamed x10 -> x6, local copies, waits for them, and re-layouts: 4.48 us -> 3.18 us
where the time goes in v4:
time: 114 us
  Pallas kernels  107 us (94%)
  local copies, waits for them, and re-layouts  3.28 us (3%)
  other arithmetic  3.04 us (3%)
    pallas_call x2, Pallas kernels, per_device(): pl.pallas_call(functools.partial(product_kernel, first, n_row, n_col, pie...  84.5 us
    pallas_call x1, Pallas kernels, per_device(): pl.pallas_call(functools.partial(factor_kernel, n_row, n_col, order), out...  12.7 us
    pallas_call x2, Pallas kernels, per_device(): pl.pallas_call(functools.partial(sum_kernel, n_col), out_shape=(shape((pa...  7.92 us
    unnamed x6, local copies, waits for them, and re-layouts  3.18 us

profile of v4, /device:TPU:0, one launch (start us, length us, event | category | flops | bytes accessed | tf_op | source)
XLA Modules:
  0.0 114.3 jit_solution(8349092761850100353)
XLA Ops:
  0.7 0.7 and_select_fusion.1
  1.3 0.7 fusion.3
  2.0 0.2 convert_reduce_fusion
  2.2 0.7 fusion.2
  2.8 0.8 select_reduce_fusion
  3.7 0.1 reduce_sum.43
  3.8 0.0 copy-start
  3.8 1.6 %copy-done = bf16[64,128,128]{2,1,0:T(8,128)(2,1)S(1)} copy-done((bf16[64,128,128]{2,1,0:T(8,128)(2,1)S(1)}, bf16[64,128,128]{2,1,0:T(8,128)(2,1)}, u32[]{:S(2)}) %copy-start) | copy-done | bytes 2097176
  5.4 0.0 copy-start.2
  5.4 1.6 %copy-done.2 = f32[32,16384]{1,0:T(8,128)S(1)} copy-done((f32[32,16384]{1,0:T(8,128)S(1)}, f32[32,16384]{1,0:T(8,128)}, u32[]{:S(2)}) %copy-start.2) | copy-done | bytes 2097176
  7.0 0.0 copy-start.1
  7.0 39.5 %shard_map.55 = (s32[16,1,128]{2,1,0:T(1,128)S(1)}, s32[2,1,128]{2,1,0:T(1,128)S(1)}, bf16[16,4,32,128]{3,2,1,0:T(8,128)(2,1)S(1)}, bf16[2,4,16,32,128]{4,3,2,1,0:T(8,128)(2,1)S(1)}) custom-call(s32[16,1,128]{2,1,0:T(1,128)S(1)} %pad.8.refs_0_, s32[1,1,128]{2,1,0:T(1,128)S(1)} %pad.9.refs_1_, s32[64]{0:T(128)S(1)} %get-tuple-element.25.refs_2_, ...), custom_call_target="tpu_custom_call" | custom-call | tf_op jit(solution)/shard_map/pallas_call | solution.py:410
  46.5 4.0 %shard_map.56 = (f32[128,32,128]{2,1,0:T(8,128)S(1)}, f32[8,128]{1,0:T(8,128)S(1)}) custom-call(s32[16,1,128]{2,1,0:T(1,128)S(1)} %get-tuple-element.15.wanted.refs_0_, s32[2,1,128]{2,1,0:T(1,128)S(1)} %get-tuple-element.16.all_cols.refs_1_, bf16[64,32,128]{2,1,0:T(8,128)(2,1)S(1)} %bitcast.22, bf16[2,64,32,128]{3,2,1,0:T(8,128)(2,1)S(1)} %bitcast.20), custom_call_target="tpu_custom_call" | custom-call | tf_op jit(solution)/shard_map/pallas_call | solution.py:459
  50.5 0.0 copy-done.1
  50.5 45.0 %shard_map.57 = (bf16[16,4,32,128]{3,2,1,0:T(8,128)(2,1)S(1)}, bf16[2,4,16,32,128]{4,3,2,1,0:T(8,128)(2,1)S(1)}) custom-call(s32[16,1,128]{2,1,0:T(1,128)S(1)} %get-tuple-element.15.wanted.refs_0_, s32[2,1,128]{2,1,0:T(1,128)S(1)} %get-tuple-element.16.all_cols.refs_1_, s32[64]{0:T(128)S(1)} %get-tuple-element.25.refs_2_, s32[64]{0:T(128)S(1)} %get-tuple-element.26.refs_3_, ...), custom_call_target="tpu_custom_call" | custom-call | tf_op jit(solution)/shard_map/pallas_call | solution.py:410
  95.5 4.0 %shard_map.58 = (f32[128,32,128]{2,1,0:T(8,128)S(1)}, f32[8,128]{1,0:T(8,128)S(1)}) custom-call(s32[16,1,128]{2,1,0:T(1,128)S(1)} %get-tuple-element.15.wanted.refs_0_, s32[2,1,128]{2,1,0:T(1,128)S(1)} %get-tuple-element.16.all_cols.refs_1_, bf16[64,32,128]{2,1,0:T(8,128)(2,1)S(1)} %bitcast.21, bf16[2,64,32,128]{3,2,1,0:T(8,128)(2,1)S(1)} %bitcast.19), custom_call_target="tpu_custom_call" | custom-call | tf_op jit(solution)/shard_map/pallas_call | solution.py:459
  99.5 12.7 %shard_map.59.inverse = f32[32,32]{1,0:T(8,128)S(1)} custom-call(f32[8,128]{1,0:T(8,128)S(1)} %get-tuple-element.24.gram), custom_call_target="tpu_custom_call" | custom-call | tf_op jit(solution)/shard_map/pallas_call | solution.py:476
  112.2 2.1 %shard_map.60 = f32[32,16384]{1,0:T(8,128)} custom-call(f32[128,32,128]{2,1,0:T(8,128)S(1)} %get-tuple-element.23.source, f32[32,32]{1,0:T(8,128)S(1)} %shard_map.59.inverse), custom_call_target="tpu_custom_call" | custom-call | tf_op jit(solution)/shard_map/pallas_call | solution.py:486
  (4 shorter events, 0.1 us)
Async XLA Ops:
  3.8 1.6 %copy-start = (bf16[64,128,128]{2,1,0:T(8,128)(2,1)S(1)}, bf16[64,128,128]{2,1,0:T(8,128)(2,1)}, u32[]{:S(2)}) copy-start(bf16[64,128,128]{2,1,0:T(8,128)(2,1)} %refs_7_.1) | copy-start | bytes 6291460
  5.4 1.6 %copy-start.2 = (f32[32,16384]{1,0:T(8,128)S(1)}, f32[32,16384]{1,0:T(8,128)}, u32[]{:S(2)}) copy-start(f32[32,16384]{1,0:T(8,128)} %refs_5_.1) | copy-start | bytes 6291460
  7.0 43.5 %copy-start.1 = (bf16[64,128,128]{2,1,0:T(8,128)(2,1)S(1)}, bf16[64,128,128]{2,1,0:T(8,128)(2,1)}, u32[]{:S(2)}) copy-start(bf16[64,128,128]{2,1,0:T(8,128)(2,1)} %refs_7_.1) | copy-start | bytes 6291460
